TPU v7x, 256 devices: a whole 4x4x8 slice. The times are simulated.
256 devices in a mesh: frame: 64 (over z_lo, y, x), row: 4 (over z_hi, core).
Axes of the slice: x: 4, y: 4, z: 8 (z_hi: 2, z_lo: 4; z = z_hi * 4 + z_lo), core: 2. Of those that a mesh axis runs over, the one named last changes fastest.
Arguments:
- clip: bfloat16 [128, 48, 128, 320], P('frame', 'row'), may hold values from -6 to 6
- w_spatial: bfloat16 [3, 3, 320, 320], replicated, may hold values from -0.109375 to 0.109375
- b_spatial: float32 [320], replicated, may hold values from -3 to 3
- w_temporal: bfloat16 [3, 320, 320], replicated, may hold values from -0.1875 to 0.1875
- b_temporal: float32 [320], replicated, may hold values from -3 to 3
- ln_gain: float32 [320], replicated, may hold values from 0.1 to 1.9
- ln_bias: float32 [320], replicated, may hold values from -3 to 3
- w_query: bfloat16 [320, 320], replicated, may hold values from -1.677051 to 1.677051
- w_key: bfloat16 [320, 320], replicated, may hold values from -1.677051 to 1.677051
- w_value: bfloat16 [320, 320], replicated, may hold values from -0.3125 to 0.3125
- w_out: bfloat16 [320, 320], replicated, may hold values from -0.3125 to 0.3125
- b_out: float32 [320], replicated, may hold values from -3 to 3
Outputs:
- mixed: bfloat16 [128, 48, 128, 320], P('frame', 'row')
All inputs are finite; a program needn't handle non-finite values.
Results may differ from a plain program's by a relative error of at most 0.0062.
Values may be sent and summed in bfloat16 or wider, within the bound.
No kernel may reach another device: no remote copies, remote signals or barrier semaphores. Data moves between devices by JAX's collectives and lax.ppermute only.
A program may use at most 128 MiB of HBM per device.

v0:
```python
import functools

import jax
import jax.numpy as jnp
from jax import lax
from jax.experimental import pallas as pl
from jax.experimental.pallas import tpu as pltpu
from jax.sharding import PartitionSpec as P


BF = jnp.bfloat16
F32 = jnp.float32
C = 320
CP = 384
LANES = 640
CHUNK = 4
GROUP = 8
UA = 4
UB = 1024
UC = 4
EXP_SCALE = 0.125 * 1.4426950408889634


def shift_rows(value, step):
    count = value.shape[0]
    turned = pltpu.roll(value, step % count, 0)
    row = lax.broadcasted_iota(jnp.int32, value.shape, 0)
    edge = 0 if step == 1 else count - 1
    return jnp.where(row == edge, 0.0, turned)


def conv_kernel(parts, rows, w_hbm, b_ref, x_hbm, low_hbm, high_hbm, out, *scratch):
    count = len(parts)
    strips, turned, w_ref, w_even, w_odd, x_sem, w_sem = scratch
    loads = []
    for h, chunk in enumerate(parts):
        first, last = chunk * CHUNK - 1, (chunk + 1) * CHUNK
        for f in range(2):
            pieces = [(x_hbm.at[f, max(first, 0) : min(last, rows - 1) + 1], int(first < 0))]
            if first < 0:
                pieces.append((low_hbm.at[f], 0))
            if last == rows:
                pieces.append((high_hbm.at[f], CHUNK + 1))
            for source, at in pieces:
                loads.append(
                    pltpu.make_async_copy(
                        source,
                        strips.at[h, f, at : at + source.shape[0]],
                        x_sem.at[len(loads)],
                    )
                )
    w_load = pltpu.make_async_copy(w_hbm, w_ref, w_sem)
    w_load.start()
    for load in loads:
        load.start()
    w_load.wait()
    w_even[960:1024, :] = jnp.zeros((64, 1024), BF)
    w_odd[0:64, :] = jnp.zeros((64, 1024), BF)
    for a in range(3):
        at = a * C
        for b in range(3):
            main = w_ref[a, b, :, 0:256]
            w_even[at : at + C, b * 256 : (b + 1) * 256] = main
            w_odd[64 + at : 64 + at + C, b * 256 : (b + 1) * 256] = main
        rest_w = jnp.concatenate(
            [w_ref[a, b, :, 256:C] for b in range(3)] + [jnp.zeros((C, 64), BF)], axis=1
        )
        w_even[at : at + C, 768:1024] = rest_w
        w_odd[64 + at : 64 + at + C, 768:1024] = rest_w
    for load in loads:
        load.wait()
    lane = lax.broadcasted_iota(jnp.int32, (128, 128), 1)
    for h in range(count):
        for f in range(2):
            turned[f] = strips[h, f].reshape((CHUNK + 2) * C, 128).T
        for odd, weights in ((0, w_even), (1, w_odd)):
            starts = (0, 640) if odd == 0 else (256, 896)
            left = jnp.concatenate(
                [turned[f, :, s : s + 1024] for s in starts for f in range(2)], axis=0
            )
            y = jnp.dot(left, weights[...], preferred_element_type=F32)
            for n in range(2):
                to = slice((odd + 2 * n) * 16, (odd + 2 * n + 1) * 16)
                tails = []
                for f in range(2):
                    at = (n * 2 + f) * 128
                    part = y[at : at + 128]
                    main = (
                        shift_rows(part[:, 0:256], 1)
                        + part[:, 256:512]
                        + shift_rows(part[:, 512:768], -1)
                        + b_ref[0:1, 0:256]
                    )
                    out[to, h, :, f * 256 : (f + 1) * 256] = main.reshape(16, 8, 256).astype(BF)
                    pair = part[:, 768:896]
                    tails.append(
                        shift_rows(pair, 1)
                        + pltpu.roll(pair, 64, 1)
                        + shift_rows(part[:, 896:1024], -1)
                        + b_ref[0:1, 256:384]
                    )
                tail = jnp.where(lane < 64, tails[0], pltpu.roll(tails[1], 64, 1))
                out[to, h, :, 512:640] = tail.reshape(16, 8, 128).astype(BF)


def spatial_chunk(parts, low, x, high, w, b):
    count = len(parts)
    rows = x.shape[1]
    shape = (64, count, 8, LANES)
    far = pl.BlockSpec(memory_space=pltpu.HBM)
    if parts[0] > 0:
        low = x
    if (parts[-1] + 1) * CHUNK < rows:
        high = x
    return pl.pallas_call(
        functools.partial(conv_kernel, parts, rows),
        out_shape=jax.ShapeDtypeStruct(shape, BF),
        grid=(1,),
        in_specs=[far, full((1, CP)), far, far, far],
        out_specs=full(shape),
        scratch_shapes=[
            pltpu.VMEM((count, 2, CHUNK + 2, C, 128), BF),
            pltpu.VMEM((2, 128, (CHUNK + 2) * C), BF),
            pltpu.VMEM((3, 3, C, C), BF),
            pltpu.VMEM((1024, 1024), BF),
            pltpu.VMEM((1024, 1024), BF),
            pltpu.SemaphoreType.DMA((4 * count,)),
            pltpu.SemaphoreType.DMA,
        ],
        compiler_params=pltpu.CompilerParams(vmem_limit_bytes=32 << 20),
        cost_estimate=pl.CostEstimate(
            flops=2200000000 * count, transcendentals=0, bytes_accessed=4000000 * count
        ),
        name="spatial",
    )(w, b, x, low, high)


def full(block):
    return pl.BlockSpec(block, lambda i: (0,) * len(block))


def attend_kernel(
    x_ref, we_hbm, wo_hbm, vector_ref, wqkv_hbm, wout_hbm, out_ref, *rest
):
    *rest, we_ref, wo_ref, wqkv_ref, wout_ref, sems = rest
    loads = [
        pltpu.make_async_copy(source, target, sems.at[n])
        for n, (source, target) in enumerate(
            ((we_hbm, we_ref), (wo_hbm, wo_ref), (wqkv_hbm, wqkv_ref), (wout_hbm, wout_ref))
        )
    ]

    @pl.when(pl.program_id(0) == 0)
    def _():
        for load in loads:
            load.start()

    bt_ref, gain_ref, bias_ref, bout_ref = (vector_ref.at[i : i + 1] for i in range(4))
    xs, le, lo, fe, fo, fr, nm, qkv, at, ys, sc, ex = rest
    xs[:, 0:8, :] = jnp.zeros((5, 8, 128), F32)
    xs[:, 520:528, :] = jnp.zeros((5, 8, 128), F32)
    for c in range(5):
        piece = x_ref[:, 0, :, c * 128 : (c + 1) * 128]
        xs[c, 8:520, :] = piece.astype(F32).reshape(512, 128)
    for p in range(GROUP):
        at_rows = slice(p * 64, (p + 1) * 64)
        for c in range(5):
            here = xs[c, pl.ds(8 + p, 64, stride=8), :].astype(BF)
            le[at_rows, 384 + c * 128 : 512 + c * 128] = here
            lo[at_rows, c * 128 : (c + 1) * 128] = here
        for n, c in enumerate((2, 3, 4)):
            before = xs[c, pl.ds(p, 64, stride=8), :].astype(BF)
            le[at_rows, n * 128 : (n + 1) * 128] = before
        for n, c in enumerate((0, 1, 4)):
            after = xs[c, pl.ds(16 + p, 64, stride=8), :].astype(BF)
            lo[at_rows, 640 + n * 128 : 768 + n * 128] = after

    @pl.when(pl.program_id(0) == 0)
    def _():
        for load in loads:
            load.wait()

    fe[...] = jnp.dot(le[...], we_ref[...], preferred_element_type=F32)
    fo[...] = jnp.dot(lo[...], wo_ref[...], preferred_element_type=F32)
    lane = lax.broadcasted_iota(jnp.int32, (64, 128), 1)
    keep = lane < 64

    def norm(p, carry):
        rows64 = pl.ds(pl.multiple_of(p * 64, 64), 64)
        tail = le[rows64, 896:1024].astype(F32)
        for odd, total in ((0, fe), (1, fo)):
            main = (
                total[rows64, 0:256]
                + le[rows64, 384 + 256 * odd : 640 + 256 * odd].astype(F32)
                + bt_ref[0:1, 0:256]
            )
            mine = pltpu.roll(tail, 64, 1) if odd else tail
            rim = total[rows64, 256:384] + jnp.where(keep, mine, 0.0) + bt_ref[0:1, 256:384]
            main = main.astype(BF)
            rim = rim.astype(BF)
            rows = pl.ds(pl.multiple_of(p * 128 + odd * 64, 64), 64)
            fr[rows, 0:256] = main
            fr[rows, 256:384] = rim
            main = main.astype(F32)
            rim = rim.astype(F32)
            mean = (
                jnp.sum(main[:, 0:128] + main[:, 128:256] + rim, axis=1, keepdims=True)
            ) * (1.0 / C)
            dm = main - mean
            dr = jnp.where(keep, rim - mean, 0.0)
            square = dm * dm
            var = jnp.sum(
                square[:, 0:128] + square[:, 128:256] + dr * dr, axis=1, keepdims=True
            ) * (1.0 / C)
            scale = lax.rsqrt(var + 1e-05)
            nm[rows, 0:256] = (
                dm * scale * gain_ref[0:1, 0:256] + bias_ref[0:1, 0:256]
            ).astype(BF)
            nm[rows, 256:384] = (
                dr * scale * gain_ref[0:1, 256:384] + bias_ref[0:1, 256:384]
            ).astype(BF)
        return carry

    lax.fori_loop(0, GROUP, norm, 0)
    for half in range(2):
        rows = slice(half * 512, (half + 1) * 512)
        qkv[rows, :] = jnp.dot(nm[rows, :], wqkv_ref[...], preferred_element_type=F32).astype(BF)

    wide = lax.broadcasted_iota(jnp.int32, (128, 128), 1) < 64

    nt = (((1,), (1,)), ((), ()))

    def score(step, carry):
        for u in range(UA):
            p = step * UA + u
            rows = pl.ds(pl.multiple_of(p * 128, 128), 128)
            for pair in range(2):
                q = qkv[rows, pair * 128 : (pair + 1) * 128]
                k = qkv[rows, 256 + pair * 128 : 384 + pair * 128]
                zero = jnp.zeros_like(q)
                both = jnp.concatenate(
                    [jnp.where(wide, q, zero), jnp.where(wide, zero, q)], axis=0
                )
                to = pl.ds(pl.multiple_of(p * 640 + pair * 256, 128), 256)
                sc[to, :] = lax.dot_general(both, k, nt, preferred_element_type=F32)
            to = pl.ds(pl.multiple_of(p * 640 + 512, 128), 128)
            sc[to, :] = lax.dot_general(
                qkv[rows, 768:896], qkv[rows, 896:1024], nt, preferred_element_type=F32
            )
        return carry

    lax.fori_loop(0, GROUP // UA, score, 0)

    def raise_all(step, carry):
        rows = pl.ds(pl.multiple_of(step * UB, UB), UB)
        scores = sc[rows, :]
        top = jnp.max(scores, axis=1, keepdims=True)
        ex[rows, :] = jnp.exp2((scores - top) * EXP_SCALE).astype(BF)
        return carry

    lax.fori_loop(0, GROUP * 640 // UB, raise_all, 0)
    ones = jnp.ones((128, 128), BF)

    def gather(step, carry):
        for u in range(UC):
            p = step * UC + u
            rows = pl.ds(pl.multiple_of(p * 128, 128), 128)
            for pair in range(2):
                v = qkv[rows, 512 + pair * 128 : 640 + pair * 128]
                to = pl.ds(pl.multiple_of(p * 640 + pair * 256, 128), 256)
                out = jnp.dot(
                    ex[to, :], jnp.concatenate([v, ones], axis=1), preferred_element_type=F32
                )
                top = jnp.where(wide, out[0:128, 0:128], out[128:256, 0:128])
                under = jnp.where(wide, out[0:128, 128:256], out[128:256, 128:256])
                at[rows, pair * 128 : (pair + 1) * 128] = (top / under).astype(BF)
            to = pl.ds(pl.multiple_of(p * 640 + 512, 128), 128)
            qv = qkv[rows, 768:896]
            out = jnp.dot(
                ex[to, :], jnp.concatenate([qv, ones], axis=1), preferred_element_type=F32
            )
            at[rows, 256:384] = (out[:, 0:128] / out[:, 128:256]).astype(BF)
        return carry

    lax.fori_loop(0, GROUP // UC, gather, 0)
    for half in range(2):
        rows = slice(half * 512, (half + 1) * 512)
        y = (
            fr[rows, :].astype(F32)
            + jnp.dot(at[rows, :], wout_ref[...], preferred_element_type=F32)
            + bout_ref[0:1, :]
        )
        for j in range(4):
            p = half * 4 + j
            even = y[j * 128 : j * 128 + 64]
            odd = y[j * 128 + 64 : j * 128 + 128]
            place = pl.ds(p, 64, stride=8)
            for c in range(2):
                ys[c, place, :] = even[:, c * 128 : (c + 1) * 128]
                ys[2 + c, place, :] = odd[:, c * 128 : (c + 1) * 128]
            ys[4, place, :] = jnp.where(keep, even[:, 256:384], pltpu.roll(odd[:, 256:384], 64, 1))
    for c in range(5):
        piece = ys[c].reshape(64, 8, 128)
        out_ref[:, 0, :, c * 128 : (c + 1) * 128] = piece.astype(BF)


def attend_chunk(x, weights):
    count = x.shape[1]
    block = pl.BlockSpec((64, 1, 8, LANES), lambda i: (0, i, 0, 0))
    far = pl.BlockSpec(memory_space=pltpu.HBM)
    return pl.pallas_call(
        attend_kernel,
        out_shape=jax.ShapeDtypeStruct(x.shape, BF),
        grid=(count,),
        in_specs=[block, far, far, full(weights[2].shape), far, far],
        out_specs=block,
        scratch_shapes=[
            pltpu.VMEM((5, 528, 128), F32),
            pltpu.VMEM((512, 1024), BF),
            pltpu.VMEM((512, 1024), BF),
            pltpu.VMEM((512, CP), F32),
            pltpu.VMEM((512, CP), F32),
            pltpu.VMEM((1024, CP), BF),
            pltpu.VMEM((1024, CP), BF),
            pltpu.VMEM((1024, 1024), BF),
            pltpu.VMEM((1024, CP), BF),
            pltpu.VMEM((5, 512, 128), F32),
            pltpu.VMEM((5120, 128), F32),
            pltpu.VMEM((5120, 128), BF),
            pltpu.VMEM((1024, CP), BF),
            pltpu.VMEM((1024, CP), BF),
            pltpu.VMEM((CP, 1024), BF),
            pltpu.VMEM((CP, CP), BF),
            pltpu.SemaphoreType.DMA((4,)),
        ],
        compiler_params=pltpu.CompilerParams(vmem_limit_bytes=32 << 20),
        cost_estimate=pl.CostEstimate(
            flops=4000000000 * count, transcendentals=700000 * count, bytes_accessed=4000000 * count
        ),
        name="attend",
    )(x, *weights)


def final_kernel(x_ref, *rest):
    out = rest[-1]
    for i in range(CHUNK):
        y = x_ref[i * 16 : (i + 1) * 16, 0].reshape(128, LANES).T
        out[0, i, 0:256, :] = y[0:256]
        out[1, i, 0:256, :] = y[256:512]
        out[0, i, 256:320, :] = y[512:576]
        out[1, i, 256:320, :] = y[576:640]


def final_chunk(x, held, first, step, rows):
    count = x.shape[1]
    operands = [x]
    specs = [pl.BlockSpec((64, 1, 8, LANES), lambda i: (0, i, 0, 0))]
    aliases = {}
    if held is not None:
        operands.append(held)
        specs.append(pl.BlockSpec(memory_space=pl.ANY))
        aliases = {1: 0}
    return pl.pallas_call(
        final_kernel,
        out_shape=jax.ShapeDtypeStruct((2, rows, C, 128), BF),
        grid=(count,),
        in_specs=specs,
        out_specs=pl.BlockSpec((2, CHUNK, C, 128), lambda i: (0, first + i * step, 0, 0)),
        input_output_aliases=aliases,
        compiler_params=pltpu.CompilerParams(vmem_limit_bytes=16 << 20),
        cost_estimate=pl.CostEstimate(
            flops=0, transcendentals=0, bytes_accessed=1400000 * count
        ),
        name="final",
    )(*operands)


def widened(vector):
    return jnp.pad(vector, (0, CP - C)).reshape(1, CP)


def prepare_kernel(wt_ref, wq_ref, wk_ref, wv_ref, wo_ref, *outs):
    even, odd, qkv, mix = outs
    zero = jnp.zeros((64, CP), BF)
    side = jnp.zeros((C, 64), BF)
    wide = [jnp.concatenate([wt_ref[k], side], axis=1) for k in range(3)]
    a, b, c = 256, 320, 384
    for at, tap, low, high in (
        (0, 0, 0, a),
        (c - 64, 0, a, b),
        (c, 1, 0, a),
        (640, 2, 0, a),
        (896, 1, a, b),
        (960, 2, a, b),
    ):
        even[at : at + high - low, :] = wide[tap][low:high]
    even[a:b, :] = zero
    for at, tap, low, high in (
        (0, 0, 0, a),
        (a, 1, 0, a),
        (512, 0, a, b),
        (576, 1, a, b),
        (640, 2, 0, a),
        (896, 2, a, b),
    ):
        odd[at : at + high - low, :] = wide[tap][low:high]
    odd[960:1024, :] = zero
    qkv[C:CP, :] = jnp.zeros((64, 1024), BF)
    qkv[0:C, 0:256] = wq_ref[:, 0:256]
    qkv[0:C, 256:512] = wk_ref[:, 0:256]
    qkv[0:C, 512:768] = wv_ref[:, 0:256]
    qkv[0:C, 768:896] = jnp.concatenate([wq_ref[:, 256:C], wv_ref[:, 256:C]], axis=1)
    qkv[0:C, 896:1024] = jnp.concatenate([wk_ref[:, 256:C], side], axis=1)
    out = jnp.concatenate([wo_ref[...], side], axis=1)
    mix[0:256, :] = out[0:256]
    mix[256:320, :] = zero
    mix[320:384, :] = out[256:320]


def prepared(w_temporal, w_query, w_key, w_value, w_out):
    square = full((C, C))
    shapes = ((1024, CP), (1024, CP), (CP, 1024), (CP, CP))
    return pl.pallas_call(
        prepare_kernel,
        out_shape=[pltpu.HBM(shape, BF) for shape in shapes],
        grid=(1,),
        in_specs=[full((3, C, C)), square, square, square, square],
        out_specs=[full(shape) for shape in shapes],
        compiler_params=pltpu.CompilerParams(vmem_limit_bytes=16 << 20),
        cost_estimate=pl.CostEstimate(flops=0, transcendentals=0, bytes_accessed=5000000),
        name="prepare",
    )(w_temporal, w_query, w_key, w_value, w_out)


def on_device(
    clip,
    w_spatial,
    b_spatial,
    w_temporal,
    b_temporal,
    ln_gain,
    ln_bias,
    w_query,
    w_key,
    w_value,
    w_out,
    b_out,
):
    rows = clip.shape[1]
    x = jnp.transpose(clip, (0, 1, 3, 2))
    row_count = lax.axis_size("row")
    forward = [(i, i + 1) for i in range(row_count - 1)]
    backward = [(b, a) for a, b in forward]
    low = lax.ppermute(x[:, rows - 1 :], "row", forward)
    high = lax.ppermute(x[:, :1], "row", backward)
    x = pltpu.with_memory_space_constraint(x, pltpu.HBM)
    w_spatial = pltpu.with_memory_space_constraint(w_spatial, pltpu.HBM)
    bias = widened(b_spatial)
    w_even, w_odd, w_qkv, w_mix = prepared(w_temporal, w_query, w_key, w_value, w_out)
    vectors = jnp.pad(jnp.stack([b_temporal, ln_gain, ln_bias, b_out]), ((0, 4), (0, CP - C)))
    w_even, w_odd, w_qkv, w_mix = (
        pltpu.with_memory_space_constraint(w, pltpu.HBM) for w in (w_even, w_odd, w_qkv, w_mix)
    )
    weights = (w_even, w_odd, vectors, w_qkv, w_mix)

    def exchange(value):
        return lax.all_to_all(value, "frame", split_axis=0, concat_axis=0, tiled=True)

    held = None
    for parts in ((1,), (0, 2)):
        sent = spatial_chunk(parts, low, x, high, w_spatial, bias)
        sent = exchange(sent)
        sent = attend_chunk(sent, weights)
        sent = exchange(sent)
        held = final_chunk(sent, held, parts[0], parts[-1] - parts[0], rows)
    return jnp.transpose(held, (0, 1, 3, 2))


def solution(mesh):
    placed = (P("frame", "row", None, None),) + (P(),) * 11
    return jax.shard_map(
        on_device,
        mesh=mesh,
        in_specs=placed,
        out_specs=P("frame", "row", None, None),
        check_vma=False,
    )
```

profile of v0, /device:TPU:1, one launch (start us, length us, event | category | flops | bytes accessed | tf_op | source)
XLA Modules:
  0.0 154.2 jit_solution(2215848968378062936)
XLA Ops:
  0.0 0.7 pad.8
  0.7 5.4 %spatial.3 = bf16[64,1,8,640]{3,2,1,0:T(8,128)(2,1)} custom-call(bf16[3,3,320,320]{3,2,1,0:T(8,128)(2,1)} %w_hbm.3, f32[1,384]{1,0:T(1,128)S(1)} %reshape.3.b_ref, bf16[2,12,320,128]{3,2,1,0:T(8,128)(2,1)} %bitcast.2, bf16[2,12,320,128]{3,2,1,0:T(8,128)(2,1)} %bitcast.3, bf16[2,12,320,128]{3,2,1,0:T(8,128)(2,1)} %bitcast.4), custom_call_target="tpu_custom_call" | custom-call | flops 2200000000 | bytes 4000000 | tf_op jit(solution)/shard_map/spatial/pallas_call | solution.py:115
  6.1 12.5 %all-to-all-start.2 = ((bf16[64,1,8,640]{3,2,1,0:T(8,128)(2,1)}), bf16[64,1,8,640]{3,2,1,0:T(8,128)(2,1)S(1)}, u32[]{:S(2)}, u32[]{:S(2)}) async-start(bf16[64,1,8,640]{3,2,1,0:T(8,128)(2,1)} %spatial.3), calls=%async_computation.2 | async-start | bytes 1310720 | tf_op jit(solution)/shard_map/all_to_all | solution.py:467
  18.7 1.0 fusion
  19.7 7.0 %collective-permute-start = (bf16[2,1,320,128]{3,2,1,0:T(8,128)(2,1)S(1)}, bf16[2,1,320,128]{3,2,1,0:T(8,128)(2,1)S(1)}, u32[]{:S(2)}, u32[]{:S(2)}) collective-permute-start(bf16[2,1,320,128]{3,2,1,0:T(8,128)(2,1)S(1)} %get-tuple-element.14), channel_id=1, source_target_pairs={{0,1},{1,2},{2,3},{4,5},{5,6},{6,7},{8,9},{9,10},{10,11},{12,13},{... | collective-permute-start | bytes 491528 | tf_op jit(solution)/shard_map/ppermute | solution.py:454
  26.7 1.9 %collective-permute-start.1 = (bf16[2,1,320,128]{3,2,1,0:T(8,128)(2,1)S(1)}, bf16[2,1,320,128]{3,2,1,0:T(8,128)(2,1)S(1)}, u32[]{:S(2)}, u32[]{:S(2)}) collective-permute-start(bf16[2,1,320,128]{3,2,1,0:T(8,128)(2,1)S(1)} %get-tuple-element.13), channel_id=1, source_target_pairs={{1,0},{2,1},{3,2},{5,4},{6,5},{7,6},{9,8},{10,9},{11,10},{13,12},{... | collective-permute-start | bytes 491528 | tf_op jit(solution)/shard_map/ppermute | solution.py:455
  28.6 2.6 %collective-permute-done.low_hbm = bf16[2,1,320,128]{3,2,1,0:T(8,128)(2,1)S(1)} collective-permute-done((bf16[2,1,320,128]{3,2,1,0:T(8,128)(2,1)S(1)}, bf16[2,1,320,128]{3,2,1,0:T(8,128)(2,1)S(1)}, u32[]{:S(2)}, u32[]{:S(2)}) %collective-permute-start) | collective-permute-done | bytes 163872 | tf_op jit(solution)/shard_map/ppermute | solution.py:454
  31.2 7.1 %collective-permute-done.1.high_hbm = bf16[2,1,320,128]{3,2,1,0:T(8,128)(2,1)S(1)} collective-permute-done((bf16[2,1,320,128]{3,2,1,0:T(8,128)(2,1)S(1)}, bf16[2,1,320,128]{3,2,1,0:T(8,128)(2,1)S(1)}, u32[]{:S(2)}, u32[]{:S(2)}) %collective-permute-start.1) | collective-permute-done | bytes 163872 | tf_op jit(solution)/shard_map/ppermute | solution.py:455
  38.4 7.9 %spatial.2 = bf16[64,2,8,640]{3,2,1,0:T(8,128)(2,1)} custom-call(bf16[3,3,320,320]{3,2,1,0:T(8,128)(2,1)} %w_hbm.3, f32[1,384]{1,0:T(1,128)S(1)} %reshape.3.b_ref, bf16[2,12,320,128]{3,2,1,0:T(8,128)(2,1)} %bitcast.6, bf16[2,1,320,128]{3,2,1,0:T(8,128)(2,1)S(1)} %collective-permute-done.low_hbm, bf16[2,1,320,128]{3,2,1,0:T(8,128)(2,1)S(1)} %collective-permute-done.1.high_hbm), custom_call_target="tpu_custom_call" | custom-call | flops 4400000000 | bytes 8000000 | tf_op jit(solution)/shard_map/spatial/pallas_call | solution.py:115
  46.3 0.0 copy-start.5
  46.3 0.0 copy-start.6
  46.3 0.0 copy-start.7
  46.3 0.0 copy-start.8
  46.3 0.0 copy-start
  46.3 0.0 copy-start.1
  46.3 0.0 copy-start.2
  46.4 0.0 copy-start.3
  46.4 0.0 all-to-all-done.2.x_ref
  46.4 11.1 %all-to-all-start = ((bf16[64,2,8,640]{3,2,1,0:T(8,128)(2,1)}), bf16[64,2,8,640]{3,2,1,0:T(8,128)(2,1)S(1)}, u32[]{:S(2)}, u32[]{:S(2)}) async-start(bf16[64,2,8,640]{3,2,1,0:T(8,128)(2,1)} %spatial.2), calls=%async_computation | async-start | bytes 2621440 | tf_op jit(solution)/shard_map/all_to_all | solution.py:467
  57.5 0.0 copy-done.5
  57.5 0.0 copy-done.6
  57.5 0.0 copy-done.7
  57.6 0.0 copy-done.8
  57.6 0.0 copy-done
  57.6 0.0 copy-done.1
  57.6 0.0 copy-done.2
  57.6 0.0 copy-done.3
  57.6 0.0 copy-start.4
  57.6 0.9 copy-done.4
  58.6 1.7 %prepare.1 = (bf16[1024,384]{1,0:T(8,128)(2,1)}, bf16[1024,384]{1,0:T(8,128)(2,1)}, bf16[384,1024]{1,0:T(8,128)(2,1)}, bf16[384,384]{1,0:T(8,128)(2,1)}) custom-call(bf16[3,320,320]{2,1,0:T(8,128)(2,1)S(1)} %copy-done, bf16[320,320]{1,0:T(8,128)(2,1)S(1)} %copy-done.1, bf16[320,320]{1,0:T(8,128)(2,1)S(1)} %copy-done.2, bf16[320,320]{1,0:T(8,128)(2,1)S(1)} %copy-done.3, ...), custom_call_target="tpu_custom_call" | custom-call | bytes 5000000 | tf_op jit(solution)/shard_map/prepare/pallas_call | solution.py:423
  60.3 10.8 %attend.3 = bf16[64,1,8,640]{3,2,1,0:T(8,128)(2,1)} custom-call(bf16[64,1,8,640]{3,2,1,0:T(8,128)(2,1)S(1)} %all-to-all-done.2.x_ref, bf16[1024,384]{1,0:T(8,128)(2,1)} %get-tuple-element.9.we_hbm, bf16[1024,384]{1,0:T(8,128)(2,1)} %get-tuple-element.10.wo_hbm, f32[8,384]{1,0:T(8,128)S(1)} %select_maximum_fusion.vector_ref, ...), custom_call_target="tpu_custom_call" | custom-call | flops 4000000000 | bytes 4000000 | tf_op jit(solution)/shard_map/attend/pallas_call | solution.py:311
  71.1 12.9 %all-to-all-done.x_ref = bf16[64,2,8,640]{3,2,1,0:T(8,128)(2,1)S(1)} async-done(((bf16[64,2,8,640]{3,2,1,0:T(8,128)(2,1)}), bf16[64,2,8,640]{3,2,1,0:T(8,128)(2,1)S(1)}, u32[]{:S(2)}, u32[]{:S(2)}) %all-to-all-start) | async-done | bytes 1310752 | tf_op jit(solution)/shard_map/all_to_all | solution.py:467
  84.0 4.6 %all-to-all-start.3 = ((bf16[64,1,8,640]{3,2,1,0:T(8,128)(2,1)}), bf16[64,1,8,640]{3,2,1,0:T(8,128)(2,1)S(1)}, u32[]{:S(2)}, u32[]{:S(2)}) async-start(bf16[64,1,8,640]{3,2,1,0:T(8,128)(2,1)} %attend.3), calls=%async_computation.3 | async-start | bytes 1310720 | tf_op jit(solution)/shard_map/all_to_all | solution.py:467
  88.6 20.1 %attend.2 = bf16[64,2,8,640]{3,2,1,0:T(8,128)(2,1)} custom-call(bf16[64,2,8,640]{3,2,1,0:T(8,128)(2,1)S(1)} %all-to-all-done.x_ref, bf16[1024,384]{1,0:T(8,128)(2,1)} %get-tuple-element.9.we_hbm, bf16[1024,384]{1,0:T(8,128)(2,1)} %get-tuple-element.10.wo_hbm, f32[8,384]{1,0:T(8,128)S(1)} %select_maximum_fusion.vector_ref, ...), custom_call_target="tpu_custom_call" | custom-call | flops 8000000000 | bytes 8000000 | tf_op jit(solution)/shard_map/attend/pallas_call | solution.py:311
  108.8 0.0 all-to-all-done.3.x_ref
  108.8 10.2 %all-to-all-start.1 = ((bf16[64,2,8,640]{3,2,1,0:T(8,128)(2,1)}), bf16[64,2,8,640]{3,2,1,0:T(8,128)(2,1)S(1)}, u32[]{:S(2)}, u32[]{:S(2)}) async-start(bf16[64,2,8,640]{3,2,1,0:T(8,128)(2,1)} %attend.2), calls=%async_computation.1 | async-start | bytes 2621440 | tf_op jit(solution)/shard_map/all_to_all | solution.py:467
  119.0 1.1 final.2.rest_0_
  120.1 32.7 %all-to-all-done.1.x_ref = bf16[64,2,8,640]{3,2,1,0:T(8,128)(2,1)S(1)} async-done(((bf16[64,2,8,640]{3,2,1,0:T(8,128)(2,1)}), bf16[64,2,8,640]{3,2,1,0:T(8,128)(2,1)S(1)}, u32[]{:S(2)}, u32[]{:S(2)}) %all-to-all-start.1) | async-done | bytes 1310752 | tf_op jit(solution)/shard_map/all_to_all | solution.py:467
  152.7 1.4 final.3
  (6 shorter events, 0.0 us)
Async XLA Ops:
  6.1 40.2 %all-to-all-start.2 = ((bf16[64,1,8,640]{3,2,1,0:T(8,128)(2,1)}), bf16[64,1,8,640]{3,2,1,0:T(8,128)(2,1)S(1)}, u32[]{:S(2)}, u32[]{:S(2)}) async-start(bf16[64,1,8,640]{3,2,1,0:T(8,128)(2,1)} %spatial.3), calls=%async_computation.2 | async-start | bytes 1310720 | tf_op jit(solution)/shard_map/all_to_all | solution.py:467
  19.7 11.5 %collective-permute-start = (bf16[2,1,320,128]{3,2,1,0:T(8,128)(2,1)S(1)}, bf16[2,1,320,128]{3,2,1,0:T(8,128)(2,1)S(1)}, u32[]{:S(2)}, u32[]{:S(2)}) collective-permute-start(bf16[2,1,320,128]{3,2,1,0:T(8,128)(2,1)S(1)} %get-tuple-element.14), channel_id=1, source_target_pairs={{0,1},{1,2},{2,3},{4,5},{5,6},{6,7},{8,9},{9,10},{10,11},{12,13},{... | collective-permute-start | bytes 491528 | tf_op jit(solution)/shard_map/ppermute | solution.py:454
  26.7 11.7 %collective-permute-start.1 = (bf16[2,1,320,128]{3,2,1,0:T(8,128)(2,1)S(1)}, bf16[2,1,320,128]{3,2,1,0:T(8,128)(2,1)S(1)}, u32[]{:S(2)}, u32[]{:S(2)}) collective-permute-start(bf16[2,1,320,128]{3,2,1,0:T(8,128)(2,1)S(1)} %get-tuple-element.13), channel_id=1, source_target_pairs={{1,0},{2,1},{3,2},{5,4},{6,5},{7,6},{9,8},{10,9},{11,10},{13,12},{... | collective-permute-start | bytes 491528 | tf_op jit(solution)/shard_map/ppermute | solution.py:455
  46.3 11.2 %copy-start.5 = (f32[320]{0:T(512)S(1)}, f32[320]{0:T(512)}, u32[]{:S(2)}) copy-start(f32[320]{0:T(512)} %param.16) | copy-start | bytes 3844
  46.3 11.2 %copy-start.6 = (f32[320]{0:T(512)S(1)}, f32[320]{0:T(512)}, u32[]{:S(2)}) copy-start(f32[320]{0:T(512)} %param.17) | copy-start | bytes 3844
  46.3 11.2 %copy-start.7 = (f32[320]{0:T(512)S(1)}, f32[320]{0:T(512)}, u32[]{:S(2)}) copy-start(f32[320]{0:T(512)} %param.18) | copy-start | bytes 3844
  46.3 11.2 %copy-start.8 = (f32[320]{0:T(512)S(1)}, f32[320]{0:T(512)}, u32[]{:S(2)}) copy-start(f32[320]{0:T(512)} %param.23) | copy-start | bytes 3844
  46.3 11.3 %copy-start = (bf16[3,320,320]{2,1,0:T(8,128)(2,1)S(1)}, bf16[3,320,320]{2,1,0:T(8,128)(2,1)}, u32[]{:S(2)}) copy-start(bf16[3,320,320]{2,1,0:T(8,128)(2,1)} %wt_ref.1) | copy-start | bytes 1843204
  46.3 11.3 %copy-start.1 = (bf16[320,320]{1,0:T(8,128)(2,1)S(1)}, bf16[320,320]{1,0:T(8,128)(2,1)}, u32[]{:S(2)}) copy-start(bf16[320,320]{1,0:T(8,128)(2,1)} %wq_ref.1) | copy-start | bytes 614404
  46.3 11.3 %copy-start.2 = (bf16[320,320]{1,0:T(8,128)(2,1)S(1)}, bf16[320,320]{1,0:T(8,128)(2,1)}, u32[]{:S(2)}) copy-start(bf16[320,320]{1,0:T(8,128)(2,1)} %wk_ref.1) | copy-start | bytes 614404
  46.4 11.3 %copy-start.3 = (bf16[320,320]{1,0:T(8,128)(2,1)S(1)}, bf16[320,320]{1,0:T(8,128)(2,1)}, u32[]{:S(2)}) copy-start(bf16[320,320]{1,0:T(8,128)(2,1)} %wv_ref.1) | copy-start | bytes 614404
  46.4 37.6 %all-to-all-start = ((bf16[64,2,8,640]{3,2,1,0:T(8,128)(2,1)}), bf16[64,2,8,640]{3,2,1,0:T(8,128)(2,1)S(1)}, u32[]{:S(2)}, u32[]{:S(2)}) async-start(bf16[64,2,8,640]{3,2,1,0:T(8,128)(2,1)} %spatial.2), calls=%async_computation | async-start | bytes 2621440 | tf_op jit(solution)/shard_map/all_to_all | solution.py:467
  57.6 0.9 copy-start.4
  84.0 24.8 %all-to-all-start.3 = ((bf16[64,1,8,640]{3,2,1,0:T(8,128)(2,1)}), bf16[64,1,8,640]{3,2,1,0:T(8,128)(2,1)S(1)}, u32[]{:S(2)}, u32[]{:S(2)}) async-start(bf16[64,1,8,640]{3,2,1,0:T(8,128)(2,1)} %attend.3), calls=%async_computation.3 | async-start | bytes 1310720 | tf_op jit(solution)/shard_map/all_to_all | solution.py:467
  108.8 43.9 %all-to-all-start.1 = ((bf16[64,2,8,640]{3,2,1,0:T(8,128)(2,1)}), bf16[64,2,8,640]{3,2,1,0:T(8,128)(2,1)S(1)}, u32[]{:S(2)}, u32[]{:S(2)}) async-start(bf16[64,2,8,640]{3,2,1,0:T(8,128)(2,1)} %attend.2), calls=%async_computation.1 | async-start | bytes 2621440 | tf_op jit(solution)/shard_map/all_to_all | solution.py:467
where the time goes:
time: 155 us; the launch traced here: 154 us
  waiting for transfers between devices  55.3 us (36%)
  Pallas kernels  48.5 us (31%)
  starting transfers between devices  47.4 us (31%)
  local copies, waits for them, and re-layouts  2.72 us (2%)
    all_to_all x4, waiting for transfers between devices, exchange(): lax.all_to_all(value, 'frame', split_axis=0, concat_axis=0, tiled=True)  45.6 us
    all_to_all x4, starting transfers between devices, exchange(): lax.all_to_all(value, 'frame', split_axis=0, concat_axis=0, tiled=True)  38.5 us
    pallas_call x2, Pallas kernels, attend_chunk(): pl.pallas_call(attend_kernel, out_shape=jax.ShapeDtypeStruct(x.shape, BF)...  30.9 us
    pallas_call x2, Pallas kernels, spatial_chunk(): pl.pallas_call(functools.partial(conv_kernel, parts, rows), out_shape=jax...  13.3 us
    ppermute x1, waiting for transfers between devices, on_device(): high = lax.ppermute(x[:, :1], 'row', backward)  7.14 us
    ppermute x1, starting transfers between devices, on_device(): low = lax.ppermute(x[:, rows - 1:], 'row', forward)  6.96 us
  transfers between devices with their start and end apart: 6, of which 4 were waited for; matrix products, arithmetic and copies ran while one was open for 1% of the time, Pallas kernels for 27%

commit v1 on v0

--- a/solution.py
+++ b/solution.py
@@ -15,9 +15,12 @@
 LANES = 640
 CHUNK = 4
 GROUP = 8
-UA = 4
-UB = 1024
-UC = 4
+ORDER = (
+    22, 12, 52, 3, 19, 5, 60, 58, 2, 33, 10, 8, 29, 26, 25, 9,
+    44, 18, 62, 11, 47, 40, 15, 39, 56, 57, 32, 23, 49, 43, 21, 45,
+    42, 34, 35, 46, 20, 61, 37, 14, 63, 53, 0, 38, 27, 50, 1, 55,
+    6, 13, 24, 41, 30, 28, 59, 31, 7, 16, 4, 48, 51, 54, 36, 17,
+)
 EXP_SCALE = 0.125 * 1.4426950408889634
 
 
@@ -49,14 +52,18 @@
                         x_sem.at[len(loads)],
                     )
                 )
-    w_load = pltpu.make_async_copy(w_hbm, w_ref, w_sem)
-    w_load.start()
+    w_loads = [pltpu.make_async_copy(w_hbm.at[a], w_ref.at[a], w_sem.at[a]) for a in range(3)]
+    for load in loads + w_loads:
+        load.start()
     for load in loads:
-        load.start()
-    w_load.wait()
+        load.wait()
+    for h in range(count):
+        for f in range(2):
+            turned[h, f] = strips[h, f].reshape((CHUNK + 2) * C, 128).T
     w_even[960:1024, :] = jnp.zeros((64, 1024), BF)
     w_odd[0:64, :] = jnp.zeros((64, 1024), BF)
     for a in range(3):
+        w_loads[a].wait()
         at = a * C
         for b in range(3):
             main = w_ref[a, b, :, 0:256]
@@ -67,16 +74,12 @@
         )
         w_even[at : at + C, 768:1024] = rest_w
         w_odd[64 + at : 64 + at + C, 768:1024] = rest_w
-    for load in loads:
-        load.wait()
     lane = lax.broadcasted_iota(jnp.int32, (128, 128), 1)
     for h in range(count):
-        for f in range(2):
-            turned[f] = strips[h, f].reshape((CHUNK + 2) * C, 128).T
         for odd, weights in ((0, w_even), (1, w_odd)):
             starts = (0, 640) if odd == 0 else (256, 896)
             left = jnp.concatenate(
-                [turned[f, :, s : s + 1024] for s in starts for f in range(2)], axis=0
+                [turned[h, f, :, s : s + 1024] for s in starts for f in range(2)], axis=0
             )
             y = jnp.dot(left, weights[...], preferred_element_type=F32)
             for n in range(2):
@@ -120,12 +123,12 @@
         out_specs=full(shape),
         scratch_shapes=[
             pltpu.VMEM((count, 2, CHUNK + 2, C, 128), BF),
-            pltpu.VMEM((2, 128, (CHUNK + 2) * C), BF),
+            pltpu.VMEM((count, 2, 128, (CHUNK + 2) * C), BF),
             pltpu.VMEM((3, 3, C, C), BF),
             pltpu.VMEM((1024, 1024), BF),
             pltpu.VMEM((1024, 1024), BF),
             pltpu.SemaphoreType.DMA((4 * count,)),
-            pltpu.SemaphoreType.DMA,
+            pltpu.SemaphoreType.DMA((3,)),
         ],
         compiler_params=pltpu.CompilerParams(vmem_limit_bytes=32 << 20),
         cost_estimate=pl.CostEstimate(
@@ -160,8 +163,9 @@
     xs[:, 0:8, :] = jnp.zeros((5, 8, 128), F32)
     xs[:, 520:528, :] = jnp.zeros((5, 8, 128), F32)
     for c in range(5):
-        piece = x_ref[:, 0, :, c * 128 : (c + 1) * 128]
-        xs[c, 8:520, :] = piece.astype(F32).reshape(512, 128)
+        lanes = slice(c * 128, (c + 1) * 128)
+        for j, pair in enumerate(ORDER):
+            xs[c, 8 + pair * 8 : 16 + pair * 8, :] = x_ref[j, 0, :, lanes].astype(F32)
     for p in range(GROUP):
         at_rows = slice(p * 64, (p + 1) * 64)
         for c in range(5):
@@ -230,59 +234,58 @@
 
     nt = (((1,), (1,)), ((), ()))
 
-    def score(step, carry):
-        for u in range(UA):
-            p = step * UA + u
-            rows = pl.ds(pl.multiple_of(p * 128, 128), 128)
-            for pair in range(2):
-                q = qkv[rows, pair * 128 : (pair + 1) * 128]
-                k = qkv[rows, 256 + pair * 128 : 384 + pair * 128]
-                zero = jnp.zeros_like(q)
-                both = jnp.concatenate(
-                    [jnp.where(wide, q, zero), jnp.where(wide, zero, q)], axis=0
-                )
-                to = pl.ds(pl.multiple_of(p * 640 + pair * 256, 128), 256)
-                sc[to, :] = lax.dot_general(both, k, nt, preferred_element_type=F32)
-            to = pl.ds(pl.multiple_of(p * 640 + 512, 128), 128)
-            sc[to, :] = lax.dot_general(
-                qkv[rows, 768:896], qkv[rows, 896:1024], nt, preferred_element_type=F32
+    ones = jnp.ones((128, 128), BF)
+
+    def score(p):
+        rows = pl.ds(pl.multiple_of(p * 128, 128), 128)
+        for pair in range(2):
+            q = qkv[rows, pair * 128 : (pair + 1) * 128]
+            k = qkv[rows, 256 + pair * 128 : 384 + pair * 128]
+            zero = jnp.zeros_like(q)
+            both = jnp.concatenate([jnp.where(wide, q, zero), jnp.where(wide, zero, q)], axis=0)
+            to = pl.ds(pl.multiple_of(p * 640 + pair * 256, 128), 256)
+            sc[to, :] = lax.dot_general(both, k, nt, preferred_element_type=F32)
+        to = pl.ds(pl.multiple_of(p * 640 + 512, 128), 128)
+        sc[to, :] = lax.dot_general(
+            qkv[rows, 768:896], qkv[rows, 896:1024], nt, preferred_element_type=F32
+        )
+
+    def raise_one(p):
+        for at5 in range(5):
+            rows = pl.ds(pl.multiple_of(p * 640 + at5 * 128, 128), 128)
+            scores = sc[rows, :]
+            top = jnp.max(scores, axis=1, keepdims=True)
+            ex[rows, :] = jnp.exp2((scores - top) * EXP_SCALE).astype(BF)
+
+    def gather(p):
+        rows = pl.ds(pl.multiple_of(p * 128, 128), 128)
+        for pair in range(2):
+            v = qkv[rows, 512 + pair * 128 : 640 + pair * 128]
+            to = pl.ds(pl.multiple_of(p * 640 + pair * 256, 128), 256)
+            out = jnp.dot(
+                ex[to, :], jnp.concatenate([v, ones], axis=1), preferred_element_type=F32
             )
+            top = jnp.where(wide, out[0:128, 0:128], out[128:256, 0:128])
+            under = jnp.where(wide, out[0:128, 128:256], out[128:256, 128:256])
+            at[rows, pair * 128 : (pair + 1) * 128] = (top / under).astype(BF)
+        to = pl.ds(pl.multiple_of(p * 640 + 512, 128), 128)
+        qv = qkv[rows, 768:896]
+        out = jnp.dot(ex[to, :], jnp.concatenate([qv, ones], axis=1), preferred_element_type=F32)
+        at[rows, 256:384] = (out[:, 0:128] / out[:, 128:256]).astype(BF)
+
+    def step(p, carry):
+        gather(p - 2)
+        raise_one(p - 1)
+        score(p)
         return carry
 
-    lax.fori_loop(0, GROUP // UA, score, 0)
-
-    def raise_all(step, carry):
-        rows = pl.ds(pl.multiple_of(step * UB, UB), UB)
-        scores = sc[rows, :]
-        top = jnp.max(scores, axis=1, keepdims=True)
-        ex[rows, :] = jnp.exp2((scores - top) * EXP_SCALE).astype(BF)
-        return carry
-
-    lax.fori_loop(0, GROUP * 640 // UB, raise_all, 0)
-    ones = jnp.ones((128, 128), BF)
-
-    def gather(step, carry):
-        for u in range(UC):
-            p = step * UC + u
-            rows = pl.ds(pl.multiple_of(p * 128, 128), 128)
-            for pair in range(2):
-                v = qkv[rows, 512 + pair * 128 : 640 + pair * 128]
-                to = pl.ds(pl.multiple_of(p * 640 + pair * 256, 128), 256)
-                out = jnp.dot(
-                    ex[to, :], jnp.concatenate([v, ones], axis=1), preferred_element_type=F32
-                )
-                top = jnp.where(wide, out[0:128, 0:128], out[128:256, 0:128])
-                under = jnp.where(wide, out[0:128, 128:256], out[128:256, 128:256])
-                at[rows, pair * 128 : (pair + 1) * 128] = (top / under).astype(BF)
-            to = pl.ds(pl.multiple_of(p * 640 + 512, 128), 128)
-            qv = qkv[rows, 768:896]
-            out = jnp.dot(
-                ex[to, :], jnp.concatenate([qv, ones], axis=1), preferred_element_type=F32
-            )
-            at[rows, 256:384] = (out[:, 0:128] / out[:, 128:256]).astype(BF)
-        return carry
-
-    lax.fori_loop(0, GROUP // UC, gather, 0)
+    score(0)
+    raise_one(0)
+    score(1)
+    lax.fori_loop(2, GROUP, step, 0)
+    gather(GROUP - 2)
+    raise_one(GROUP - 1)
+    gather(GROUP - 1)
     for half in range(2):
         rows = slice(half * 512, (half + 1) * 512)
         y = (
@@ -300,8 +303,9 @@
                 ys[2 + c, place, :] = odd[:, c * 128 : (c + 1) * 128]
             ys[4, place, :] = jnp.where(keep, even[:, 256:384], pltpu.roll(odd[:, 256:384], 64, 1))
     for c in range(5):
-        piece = ys[c].reshape(64, 8, 128)
-        out_ref[:, 0, :, c * 128 : (c + 1) * 128] = piece.astype(BF)
+        lanes = slice(c * 128, (c + 1) * 128)
+        for j, pair in enumerate(ORDER):
+            out_ref[j, 0, :, lanes] = ys[c, pair * 8 : pair * 8 + 8, :].astype(BF)
 
 
 def attend_chunk(x, weights):
@@ -464,7 +468,14 @@
     weights = (w_even, w_odd, vectors, w_qkv, w_mix)
 
     def exchange(value):
-        return lax.all_to_all(value, "frame", split_axis=0, concat_axis=0, tiled=True)
+        return lax.all_to_all(
+            value,
+            "frame",
+            split_axis=0,
+            concat_axis=0,
+            tiled=True,
+            axis_index_groups=[list(ORDER)],
+        )
 
     held = None
     for parts in ((1,), (0, 2)):

time: 155 us -> 147 us (0.948)
  the two profiles are of different devices: /device:TPU:1 before, /device:TPU:4 now
where the time goes in v1:
time: 147 us; the launch traced here: 144 us
  waiting for transfers between devices  61.1 us (42%)
  Pallas kernels  46.6 us (32%)
  starting transfers between devices  33.5 us (23%)
  local copies, waits for them, and re-layouts  2.72 us (2%)
    all_to_all x4, waiting for transfers between devices, exchange(): lax.all_to_all(value, 'frame', split_axis=0, concat_axis=0, tiled=True, a...  54.4 us
    all_to_all x4, starting transfers between devices, exchange(): lax.all_to_all(value, 'frame', split_axis=0, concat_axis=0, tiled=True, a...  30.9 us
    pallas_call x2, Pallas kernels, attend_chunk(): pl.pallas_call(attend_kernel, out_shape=jax.ShapeDtypeStruct(x.shape, BF)...  28.8 us
    pallas_call x2, Pallas kernels, spatial_chunk(): pl.pallas_call(functools.partial(conv_kernel, parts, rows), out_shape=jax...  13.6 us
    ppermute x1, waiting for transfers between devices, on_device(): high = lax.ppermute(x[:, :1], 'row', backward)  6.7 us
  transfers between devices with their start and end apart: 6, of which 5 were waited for; matrix products, arithmetic and copies ran while one was open for 1% of the time, Pallas kernels for 27%

profile of v1, /device:TPU:4, one launch (start us, length us, event | category | flops | bytes accessed | tf_op | source)
XLA Modules:
  0.0 144.2 jit_solution(15145357140502184926)
XLA Ops:
  0.0 0.7 pad.8
  0.7 5.6 %spatial.3 = bf16[64,1,8,640]{3,2,1,0:T(8,128)(2,1)} custom-call(bf16[3,3,320,320]{3,2,1,0:T(8,128)(2,1)} %w_hbm.3, f32[1,384]{1,0:T(1,128)S(1)} %reshape.3.b_ref, bf16[2,12,320,128]{3,2,1,0:T(8,128)(2,1)} %bitcast.2, bf16[2,12,320,128]{3,2,1,0:T(8,128)(2,1)} %bitcast.3, bf16[2,12,320,128]{3,2,1,0:T(8,128)(2,1)} %bitcast.4), custom_call_target="tpu_custom_call" | custom-call | flops 2200000000 | bytes 4000000 | tf_op jit(solution)/shard_map/spatial/pallas_call | solution.py:118
  6.3 10.4 %all-to-all-start.2 = ((bf16[64,1,8,640]{3,2,1,0:T(8,128)(2,1)}), bf16[64,1,8,640]{3,2,1,0:T(8,128)(2,1)S(1)}, u32[]{:S(2)}, u32[]{:S(2)}) async-start(bf16[64,1,8,640]{3,2,1,0:T(8,128)(2,1)} %spatial.3), calls=%async_computation.2 | async-start | bytes 1310720 | tf_op jit(solution)/shard_map/all_to_all | solution.py:471
  16.7 1.0 fusion
  17.7 1.3 collective-permute-start
  19.0 1.3 collective-permute-start.1
  20.3 0.0 collective-permute-done.low_hbm
  20.3 6.7 %collective-permute-done.1.high_hbm = bf16[2,1,320,128]{3,2,1,0:T(8,128)(2,1)S(1)} collective-permute-done((bf16[2,1,320,128]{3,2,1,0:T(8,128)(2,1)S(1)}, bf16[2,1,320,128]{3,2,1,0:T(8,128)(2,1)S(1)}, u32[]{:S(2)}, u32[]{:S(2)}) %collective-permute-start.1) | collective-permute-done | bytes 163872 | tf_op jit(solution)/shard_map/ppermute | solution.py:459
  27.0 8.1 %spatial.2 = bf16[64,2,8,640]{3,2,1,0:T(8,128)(2,1)} custom-call(bf16[3,3,320,320]{3,2,1,0:T(8,128)(2,1)} %w_hbm.3, f32[1,384]{1,0:T(1,128)S(1)} %reshape.3.b_ref, bf16[2,12,320,128]{3,2,1,0:T(8,128)(2,1)} %bitcast.6, bf16[2,1,320,128]{3,2,1,0:T(8,128)(2,1)S(1)} %collective-permute-done.low_hbm, bf16[2,1,320,128]{3,2,1,0:T(8,128)(2,1)S(1)} %collective-permute-done.1.high_hbm), custom_call_target="tpu_custom_call" | custom-call | flops 4400000000 | bytes 8000000 | tf_op jit(solution)/shard_map/spatial/pallas_call | solution.py:118
  35.1 0.0 copy-start.5
  35.1 0.0 copy-start.6
  35.1 0.0 copy-start.7
  35.1 0.0 copy-start.8
  35.1 0.0 copy-start
  35.2 0.0 copy-start.1
  35.2 0.0 copy-start.2
  35.2 0.0 copy-start.3
  35.2 3.1 %all-to-all-done.2.x_ref = bf16[64,1,8,640]{3,2,1,0:T(8,128)(2,1)S(1)} async-done(((bf16[64,1,8,640]{3,2,1,0:T(8,128)(2,1)}), bf16[64,1,8,640]{3,2,1,0:T(8,128)(2,1)S(1)}, u32[]{:S(2)}, u32[]{:S(2)}) %all-to-all-start.2) | async-done | bytes 655392 | tf_op jit(solution)/shard_map/all_to_all | solution.py:471
  38.3 6.6 %all-to-all-start = ((bf16[64,2,8,640]{3,2,1,0:T(8,128)(2,1)}), bf16[64,2,8,640]{3,2,1,0:T(8,128)(2,1)S(1)}, u32[]{:S(2)}, u32[]{:S(2)}) async-start(bf16[64,2,8,640]{3,2,1,0:T(8,128)(2,1)} %spatial.2), calls=%async_computation | async-start | bytes 2621440 | tf_op jit(solution)/shard_map/all_to_all | solution.py:471
  44.9 0.0 copy-done.5
  44.9 0.0 copy-done.6
  45.0 0.0 copy-done.7
  45.0 0.0 copy-done.8
  45.0 0.0 copy-done
  45.0 0.0 copy-done.1
  45.0 0.0 copy-done.2
  45.0 0.0 copy-done.3
  45.0 0.0 copy-start.4
  45.1 0.9 copy-done.4
  46.0 1.7 %prepare.1 = (bf16[1024,384]{1,0:T(8,128)(2,1)}, bf16[1024,384]{1,0:T(8,128)(2,1)}, bf16[384,1024]{1,0:T(8,128)(2,1)}, bf16[384,384]{1,0:T(8,128)(2,1)}) custom-call(bf16[3,320,320]{2,1,0:T(8,128)(2,1)S(1)} %copy-done, bf16[320,320]{1,0:T(8,128)(2,1)S(1)} %copy-done.1, bf16[320,320]{1,0:T(8,128)(2,1)S(1)} %copy-done.2, bf16[320,320]{1,0:T(8,128)(2,1)S(1)} %copy-done.3, ...), custom_call_target="tpu_custom_call" | custom-call | bytes 5000000 | tf_op jit(solution)/shard_map/prepare/pallas_call | solution.py:427
  47.7 10.1 %attend.3 = bf16[64,1,8,640]{3,2,1,0:T(8,128)(2,1)} custom-call(bf16[64,1,8,640]{3,2,1,0:T(8,128)(2,1)S(1)} %all-to-all-done.2.x_ref, bf16[1024,384]{1,0:T(8,128)(2,1)} %get-tuple-element.9.we_hbm, bf16[1024,384]{1,0:T(8,128)(2,1)} %get-tuple-element.10.wo_hbm, f32[8,384]{1,0:T(8,128)S(1)} %select_maximum_fusion.vector_ref, ...), custom_call_target="tpu_custom_call" | custom-call | flops 4000000000 | bytes 4000000 | tf_op jit(solution)/shard_map/attend/pallas_call | solution.py:315
  57.8 18.1 %all-to-all-done.x_ref = bf16[64,2,8,640]{3,2,1,0:T(8,128)(2,1)S(1)} async-done(((bf16[64,2,8,640]{3,2,1,0:T(8,128)(2,1)}), bf16[64,2,8,640]{3,2,1,0:T(8,128)(2,1)S(1)}, u32[]{:S(2)}, u32[]{:S(2)}) %all-to-all-start) | async-done | bytes 1310752 | tf_op jit(solution)/shard_map/all_to_all | solution.py:471
  75.9 5.2 %all-to-all-start.3 = ((bf16[64,1,8,640]{3,2,1,0:T(8,128)(2,1)}), bf16[64,1,8,640]{3,2,1,0:T(8,128)(2,1)S(1)}, u32[]{:S(2)}, u32[]{:S(2)}) async-start(bf16[64,1,8,640]{3,2,1,0:T(8,128)(2,1)} %attend.3), calls=%async_computation.3 | async-start | bytes 1310720 | tf_op jit(solution)/shard_map/all_to_all | solution.py:471
  81.2 18.7 %attend.2 = bf16[64,2,8,640]{3,2,1,0:T(8,128)(2,1)} custom-call(bf16[64,2,8,640]{3,2,1,0:T(8,128)(2,1)S(1)} %all-to-all-done.x_ref, bf16[1024,384]{1,0:T(8,128)(2,1)} %get-tuple-element.9.we_hbm, bf16[1024,384]{1,0:T(8,128)(2,1)} %get-tuple-element.10.wo_hbm, f32[8,384]{1,0:T(8,128)S(1)} %select_maximum_fusion.vector_ref, ...), custom_call_target="tpu_custom_call" | custom-call | flops 8000000000 | bytes 8000000 | tf_op jit(solution)/shard_map/attend/pallas_call | solution.py:315
  99.9 0.9 all-to-all-done.3.x_ref
  100.8 8.7 %all-to-all-start.1 = ((bf16[64,2,8,640]{3,2,1,0:T(8,128)(2,1)}), bf16[64,2,8,640]{3,2,1,0:T(8,128)(2,1)S(1)}, u32[]{:S(2)}, u32[]{:S(2)}) async-start(bf16[64,2,8,640]{3,2,1,0:T(8,128)(2,1)} %attend.2), calls=%async_computation.1 | async-start | bytes 2621440 | tf_op jit(solution)/shard_map/all_to_all | solution.py:471
  109.5 1.1 final.2.rest_0_
  110.5 32.2 %all-to-all-done.1.x_ref = bf16[64,2,8,640]{3,2,1,0:T(8,128)(2,1)S(1)} async-done(((bf16[64,2,8,640]{3,2,1,0:T(8,128)(2,1)}), bf16[64,2,8,640]{3,2,1,0:T(8,128)(2,1)S(1)}, u32[]{:S(2)}, u32[]{:S(2)}) %all-to-all-start.1) | async-done | bytes 1310752 | tf_op jit(solution)/shard_map/all_to_all | solution.py:471
  142.8 1.4 final.3
  (6 shorter events, 0.0 us)
Async XLA Ops:
  6.3 32.0 %all-to-all-start.2 = ((bf16[64,1,8,640]{3,2,1,0:T(8,128)(2,1)}), bf16[64,1,8,640]{3,2,1,0:T(8,128)(2,1)S(1)}, u32[]{:S(2)}, u32[]{:S(2)}) async-start(bf16[64,1,8,640]{3,2,1,0:T(8,128)(2,1)} %spatial.3), calls=%async_computation.2 | async-start | bytes 1310720 | tf_op jit(solution)/shard_map/all_to_all | solution.py:471
  17.7 2.6 %collective-permute-start = (bf16[2,1,320,128]{3,2,1,0:T(8,128)(2,1)S(1)}, bf16[2,1,320,128]{3,2,1,0:T(8,128)(2,1)S(1)}, u32[]{:S(2)}, u32[]{:S(2)}) collective-permute-start(bf16[2,1,320,128]{3,2,1,0:T(8,128)(2,1)S(1)} %get-tuple-element.14), channel_id=1, source_target_pairs={{0,1},{1,2},{2,3},{4,5},{5,6},{6,7},{8,9},{9,10},{10,11},{12,13},{... | collective-permute-start | bytes 491528 | tf_op jit(solution)/shard_map/ppermute | solution.py:458
  19.0 8.0 %collective-permute-start.1 = (bf16[2,1,320,128]{3,2,1,0:T(8,128)(2,1)S(1)}, bf16[2,1,320,128]{3,2,1,0:T(8,128)(2,1)S(1)}, u32[]{:S(2)}, u32[]{:S(2)}) collective-permute-start(bf16[2,1,320,128]{3,2,1,0:T(8,128)(2,1)S(1)} %get-tuple-element.13), channel_id=1, source_target_pairs={{1,0},{2,1},{3,2},{5,4},{6,5},{7,6},{9,8},{10,9},{11,10},{13,12},{... | collective-permute-start | bytes 491528 | tf_op jit(solution)/shard_map/ppermute | solution.py:459
  35.1 9.8 %copy-start.5 = (f32[320]{0:T(512)S(1)}, f32[320]{0:T(512)}, u32[]{:S(2)}) copy-start(f32[320]{0:T(512)} %param.16) | copy-start | bytes 3844
  35.1 9.8 %copy-start.6 = (f32[320]{0:T(512)S(1)}, f32[320]{0:T(512)}, u32[]{:S(2)}) copy-start(f32[320]{0:T(512)} %param.17) | copy-start | bytes 3844
  35.1 9.9 %copy-start.7 = (f32[320]{0:T(512)S(1)}, f32[320]{0:T(512)}, u32[]{:S(2)}) copy-start(f32[320]{0:T(512)} %param.18) | copy-start | bytes 3844
  35.1 9.9 %copy-start.8 = (f32[320]{0:T(512)S(1)}, f32[320]{0:T(512)}, u32[]{:S(2)}) copy-start(f32[320]{0:T(512)} %param.23) | copy-start | bytes 3844
  35.1 9.9 %copy-start = (bf16[3,320,320]{2,1,0:T(8,128)(2,1)S(1)}, bf16[3,320,320]{2,1,0:T(8,128)(2,1)}, u32[]{:S(2)}) copy-start(bf16[3,320,320]{2,1,0:T(8,128)(2,1)} %wt_ref.1) | copy-start | bytes 1843204
  35.2 9.9 %copy-start.1 = (bf16[320,320]{1,0:T(8,128)(2,1)S(1)}, bf16[320,320]{1,0:T(8,128)(2,1)}, u32[]{:S(2)}) copy-start(bf16[320,320]{1,0:T(8,128)(2,1)} %wq_ref.1) | copy-start | bytes 614404
  35.2 9.9 %copy-start.2 = (bf16[320,320]{1,0:T(8,128)(2,1)S(1)}, bf16[320,320]{1,0:T(8,128)(2,1)}, u32[]{:S(2)}) copy-start(bf16[320,320]{1,0:T(8,128)(2,1)} %wk_ref.1) | copy-start | bytes 614404
  35.2 9.9 %copy-start.3 = (bf16[320,320]{1,0:T(8,128)(2,1)S(1)}, bf16[320,320]{1,0:T(8,128)(2,1)}, u32[]{:S(2)}) copy-start(bf16[320,320]{1,0:T(8,128)(2,1)} %wv_ref.1) | copy-start | bytes 614404
  38.3 37.6 %all-to-all-start = ((bf16[64,2,8,640]{3,2,1,0:T(8,128)(2,1)}), bf16[64,2,8,640]{3,2,1,0:T(8,128)(2,1)S(1)}, u32[]{:S(2)}, u32[]{:S(2)}) async-start(bf16[64,2,8,640]{3,2,1,0:T(8,128)(2,1)} %spatial.2), calls=%async_computation | async-start | bytes 2621440 | tf_op jit(solution)/shard_map/all_to_all | solution.py:471
  45.0 0.9 copy-start.4
  75.9 24.9 %all-to-all-start.3 = ((bf16[64,1,8,640]{3,2,1,0:T(8,128)(2,1)}), bf16[64,1,8,640]{3,2,1,0:T(8,128)(2,1)S(1)}, u32[]{:S(2)}, u32[]{:S(2)}) async-start(bf16[64,1,8,640]{3,2,1,0:T(8,128)(2,1)} %attend.3), calls=%async_computation.3 | async-start | bytes 1310720 | tf_op jit(solution)/shard_map/all_to_all | solution.py:471
  100.8 42.0 %all-to-all-start.1 = ((bf16[64,2,8,640]{3,2,1,0:T(8,128)(2,1)}), bf16[64,2,8,640]{3,2,1,0:T(8,128)(2,1)S(1)}, u32[]{:S(2)}, u32[]{:S(2)}) async-start(bf16[64,2,8,640]{3,2,1,0:T(8,128)(2,1)} %attend.2), calls=%async_computation.1 | async-start | bytes 2621440 | tf_op jit(solution)/shard_map/all_to_all | solution.py:471

commit v2 on v1

--- a/solution.py
+++ b/solution.py
@@ -15,6 +15,7 @@
 LANES = 640
 CHUNK = 4
 GROUP = 8
+NORM_UNROLL = 2
 ORDER = (
     22, 12, 52, 3, 19, 5, 60, 58, 2, 33, 10, 8, 29, 26, 25, 9,
     44, 18, 62, 11, 47, 40, 15, 39, 56, 57, 32, 23, 49, 43, 21, 45,
@@ -75,6 +76,7 @@
         w_even[at : at + C, 768:1024] = rest_w
         w_odd[64 + at : 64 + at + C, 768:1024] = rest_w
     lane = lax.broadcasted_iota(jnp.int32, (128, 128), 1)
+    rim_bias = jnp.concatenate([b_ref[0:1, 256:C], jnp.zeros((1, 64), F32)], axis=1)
     for h in range(count):
         for odd, weights in ((0, w_even), (1, w_odd)):
             starts = (0, 640) if odd == 0 else (256, 896)
@@ -100,7 +102,7 @@
                         shift_rows(pair, 1)
                         + pltpu.roll(pair, 64, 1)
                         + shift_rows(part[:, 896:1024], -1)
-                        + b_ref[0:1, 256:384]
+                        + rim_bias
                     )
                 tail = jnp.where(lane < 64, tails[0], pltpu.roll(tails[1], 64, 1))
                 out[to, h, :, 512:640] = tail.reshape(16, 8, 128).astype(BF)
@@ -119,7 +121,7 @@
         functools.partial(conv_kernel, parts, rows),
         out_shape=jax.ShapeDtypeStruct(shape, BF),
         grid=(1,),
-        in_specs=[far, full((1, CP)), far, far, far],
+        in_specs=[far, full((1, C)), far, far, far],
         out_specs=full(shape),
         scratch_shapes=[
             pltpu.VMEM((count, 2, CHUNK + 2, C, 128), BF),
@@ -160,24 +162,27 @@
 
     bt_ref, gain_ref, bias_ref, bout_ref = (vector_ref.at[i : i + 1] for i in range(4))
     xs, le, lo, fe, fo, fr, nm, qkv, at, ys, sc, ex = rest
-    xs[:, 0:8, :] = jnp.zeros((5, 8, 128), F32)
-    xs[:, 520:528, :] = jnp.zeros((5, 8, 128), F32)
     for c in range(5):
         lanes = slice(c * 128, (c + 1) * 128)
-        for j, pair in enumerate(ORDER):
-            xs[c, 8 + pair * 8 : 16 + pair * 8, :] = x_ref[j, 0, :, lanes].astype(F32)
+        for j in range(0, 64, 2):
+            piece = x_ref[j : j + 2, 0, :, lanes].astype(F32)
+            for n in range(2):
+                to = ORDER[j + n] * 8
+                xs[c, to : to + 8, :] = piece[n]
     for p in range(GROUP):
         at_rows = slice(p * 64, (p + 1) * 64)
         for c in range(5):
-            here = xs[c, pl.ds(8 + p, 64, stride=8), :].astype(BF)
+            here = xs[c, pl.ds(p, 64, stride=8), :]
+            if c >= 2:
+                before = shift_rows(here, 1).astype(BF)
+                le[at_rows, (c - 2) * 128 : (c - 1) * 128] = before
+            if c < 2 or c == 4:
+                n = min(c, 2)
+                after = shift_rows(here, -1).astype(BF)
+                lo[at_rows, 640 + n * 128 : 768 + n * 128] = after
+            here = here.astype(BF)
             le[at_rows, 384 + c * 128 : 512 + c * 128] = here
             lo[at_rows, c * 128 : (c + 1) * 128] = here
-        for n, c in enumerate((2, 3, 4)):
-            before = xs[c, pl.ds(p, 64, stride=8), :].astype(BF)
-            le[at_rows, n * 128 : (n + 1) * 128] = before
-        for n, c in enumerate((0, 1, 4)):
-            after = xs[c, pl.ds(16 + p, 64, stride=8), :].astype(BF)
-            lo[at_rows, 640 + n * 128 : 768 + n * 128] = after
 
     @pl.when(pl.program_id(0) == 0)
     def _():
@@ -189,7 +194,7 @@
     lane = lax.broadcasted_iota(jnp.int32, (64, 128), 1)
     keep = lane < 64
 
-    def norm(p, carry):
+    def norm(p):
         rows64 = pl.ds(pl.multiple_of(p * 64, 64), 64)
         tail = le[rows64, 896:1024].astype(F32)
         for odd, total in ((0, fe), (1, fo)):
@@ -223,9 +228,13 @@
             nm[rows, 256:384] = (
                 dr * scale * gain_ref[0:1, 256:384] + bias_ref[0:1, 256:384]
             ).astype(BF)
+
+    def norms(step, carry):
+        for u in range(NORM_UNROLL):
+            norm(step * NORM_UNROLL + u)
         return carry
 
-    lax.fori_loop(0, GROUP, norm, 0)
+    lax.fori_loop(0, GROUP // NORM_UNROLL, norms, 0)
     for half in range(2):
         rows = slice(half * 512, (half + 1) * 512)
         qkv[rows, :] = jnp.dot(nm[rows, :], wqkv_ref[...], preferred_element_type=F32).astype(BF)
@@ -273,16 +282,18 @@
         out = jnp.dot(ex[to, :], jnp.concatenate([qv, ones], axis=1), preferred_element_type=F32)
         at[rows, 256:384] = (out[:, 0:128] / out[:, 128:256]).astype(BF)
 
-    def step(p, carry):
-        gather(p - 2)
-        raise_one(p - 1)
-        score(p)
+    def step(n, carry):
+        for u in range(2):
+            p = n * 2 + u
+            gather(p - 2)
+            raise_one(p - 1)
+            score(p)
         return carry
 
     score(0)
     raise_one(0)
     score(1)
-    lax.fori_loop(2, GROUP, step, 0)
+    lax.fori_loop(1, GROUP // 2, step, 0)
     gather(GROUP - 2)
     raise_one(GROUP - 1)
     gather(GROUP - 1)
@@ -304,8 +315,9 @@
             ys[4, place, :] = jnp.where(keep, even[:, 256:384], pltpu.roll(odd[:, 256:384], 64, 1))
     for c in range(5):
         lanes = slice(c * 128, (c + 1) * 128)
-        for j, pair in enumerate(ORDER):
-            out_ref[j, 0, :, lanes] = ys[c, pair * 8 : pair * 8 + 8, :].astype(BF)
+        for j in range(0, 64, 2):
+            two = [ys[c, n * 8 : n * 8 + 8, :] for n in ORDER[j : j + 2]]
+            out_ref[j : j + 2, 0, :, lanes] = jnp.stack(two).astype(BF)
 
 
 def attend_chunk(x, weights):
@@ -319,7 +331,7 @@
         in_specs=[block, far, far, full(weights[2].shape), far, far],
         out_specs=block,
         scratch_shapes=[
-            pltpu.VMEM((5, 528, 128), F32),
+            pltpu.VMEM((5, 512, 128), F32),
             pltpu.VMEM((512, 1024), BF),
             pltpu.VMEM((512, 1024), BF),
             pltpu.VMEM((512, CP), F32),
@@ -377,10 +389,6 @@
         ),
         name="final",
     )(*operands)
-
-
-def widened(vector):
-    return jnp.pad(vector, (0, CP - C)).reshape(1, CP)
 
 
 def prepare_kernel(wt_ref, wq_ref, wk_ref, wv_ref, wo_ref, *outs):
@@ -459,7 +467,7 @@
     high = lax.ppermute(x[:, :1], "row", backward)
     x = pltpu.with_memory_space_constraint(x, pltpu.HBM)
     w_spatial = pltpu.with_memory_space_constraint(w_spatial, pltpu.HBM)
-    bias = widened(b_spatial)
+    bias = b_spatial.reshape(1, C)
     w_even, w_odd, w_qkv, w_mix = prepared(w_temporal, w_query, w_key, w_value, w_out)
     vectors = jnp.pad(jnp.stack([b_temporal, ln_gain, ln_bias, b_out]), ((0, 4), (0, CP - C)))
     w_even, w_odd, w_qkv, w_mix = (

time: 147 us -> 144 us (0.980)
  Pallas kernels: 46.6 us -> 42.5 us
  waiting for transfers between devices: 61.1 us -> 65.2 us
  starting transfers between devices: 33.5 us -> 30.7 us
    all_to_all x4, waiting for transfers between devices: 54.4 us -> 58.5 us  [exchange(): lax.all_to_all(value, 'frame', split_axis=0, concat_axis=0, tiled=True, a...]
    pallas_call x2, Pallas kernels: 28.8 us -> 24.7 us  [attend_chunk(): pl.pallas_call(attend_kernel, out_shape=jax.ShapeDtypeStruct(x.shape, BF)...]
    all_to_all x4, starting transfers between devices: 30.9 us -> 28.1 us  [exchange(): lax.all_to_all(value, 'frame', split_axis=0, concat_axis=0, tiled=True, a...]
  transfers between devices with their start and end apart: 6 -> 6, of which waited for: 5 -> 5; matrix products, arithmetic and copies ran while one was open for 1% -> 1% of each run, Pallas kernels for 27% -> 25%
where the time goes in v2:
time: 144 us; the launch traced here: 141 us
  waiting for transfers between devices  65.2 us (45%)
  Pallas kernels  42.5 us (30%)
  starting transfers between devices  30.7 us (21%)
  local copies, waits for them, and re-layouts  2.71 us (2%)
    all_to_all x4, waiting for transfers between devices, exchange(): lax.all_to_all(value, 'frame', split_axis=0, concat_axis=0, tiled=True, a...  58.5 us
    all_to_all x4, starting transfers between devices, exchange(): lax.all_to_all(value, 'frame', split_axis=0, concat_axis=0, tiled=True, a...  28.1 us
    pallas_call x2, Pallas kernels, attend_chunk(): pl.pallas_call(attend_kernel, out_shape=jax.ShapeDtypeStruct(x.shape, BF)...  24.7 us
    pallas_call x2, Pallas kernels, spatial_chunk(): pl.pallas_call(functools.partial(conv_kernel, parts, rows), out_shape=jax...  13.6 us
    ppermute x1, waiting for transfers between devices, on_device(): high = lax.ppermute(x[:, :1], 'row', backward)  6.7 us
  transfers between devices with their start and end apart: 6, of which 5 were waited for; matrix products, arithmetic and copies ran while one was open for 1% of the time, Pallas kernels for 25%

profile of v2, /device:TPU:4, one launch (start us, length us, event | category | flops | bytes accessed | tf_op | source)
XLA Modules:
  0.0 141.3 jit_solution(8500975217188378772)
XLA Ops:
  0.0 0.7 reshape.3.b_ref
  0.7 5.6 %spatial.3 = bf16[64,1,8,640]{3,2,1,0:T(8,128)(2,1)} custom-call(bf16[3,3,320,320]{3,2,1,0:T(8,128)(2,1)} %w_hbm.3, f32[1,320]{1,0:T(1,128)S(1)} %reshape.3.b_ref, bf16[2,12,320,128]{3,2,1,0:T(8,128)(2,1)} %bitcast.2, bf16[2,12,320,128]{3,2,1,0:T(8,128)(2,1)} %bitcast.3, bf16[2,12,320,128]{3,2,1,0:T(8,128)(2,1)} %bitcast.4), custom_call_target="tpu_custom_call" | custom-call | flops 2200000000 | bytes 4000000 | tf_op jit(solution)/shard_map/spatial/pallas_call | solution.py:120
  6.3 10.4 %all-to-all-start.2 = ((bf16[64,1,8,640]{3,2,1,0:T(8,128)(2,1)}), bf16[64,1,8,640]{3,2,1,0:T(8,128)(2,1)S(1)}, u32[]{:S(2)}, u32[]{:S(2)}) async-start(bf16[64,1,8,640]{3,2,1,0:T(8,128)(2,1)} %spatial.3), calls=%async_computation.2 | async-start | bytes 1310720 | tf_op jit(solution)/shard_map/all_to_all | solution.py:479
  16.7 1.0 fusion
  17.7 1.3 collective-permute-start
  19.0 1.3 collective-permute-start.1
  20.3 0.0 collective-permute-done.low_hbm
  20.3 6.7 %collective-permute-done.1.high_hbm = bf16[2,1,320,128]{3,2,1,0:T(8,128)(2,1)S(1)} collective-permute-done((bf16[2,1,320,128]{3,2,1,0:T(8,128)(2,1)S(1)}, bf16[2,1,320,128]{3,2,1,0:T(8,128)(2,1)S(1)}, u32[]{:S(2)}, u32[]{:S(2)}) %collective-permute-start.1) | collective-permute-done | bytes 163872 | tf_op jit(solution)/shard_map/ppermute | solution.py:467
  27.0 8.1 %spatial.2 = bf16[64,2,8,640]{3,2,1,0:T(8,128)(2,1)} custom-call(bf16[3,3,320,320]{3,2,1,0:T(8,128)(2,1)} %w_hbm.3, f32[1,320]{1,0:T(1,128)S(1)} %reshape.3.b_ref, bf16[2,12,320,128]{3,2,1,0:T(8,128)(2,1)} %bitcast.6, bf16[2,1,320,128]{3,2,1,0:T(8,128)(2,1)S(1)} %collective-permute-done.low_hbm, bf16[2,1,320,128]{3,2,1,0:T(8,128)(2,1)S(1)} %collective-permute-done.1.high_hbm), custom_call_target="tpu_custom_call" | custom-call | flops 4400000000 | bytes 8000000 | tf_op jit(solution)/shard_map/spatial/pallas_call | solution.py:120
  35.1 0.0 copy-start.5
  35.1 0.0 copy-start.6
  35.1 0.0 copy-start.7
  35.1 0.0 copy-start.8
  35.1 0.0 copy-start
  35.1 0.0 copy-start.1
  35.2 0.0 copy-start.2
  35.2 0.0 copy-start.3
  35.2 3.1 %all-to-all-done.2.x_ref = bf16[64,1,8,640]{3,2,1,0:T(8,128)(2,1)S(1)} async-done(((bf16[64,1,8,640]{3,2,1,0:T(8,128)(2,1)}), bf16[64,1,8,640]{3,2,1,0:T(8,128)(2,1)S(1)}, u32[]{:S(2)}, u32[]{:S(2)}) %all-to-all-start.2) | async-done | bytes 655392 | tf_op jit(solution)/shard_map/all_to_all | solution.py:479
  38.3 6.6 %all-to-all-start = ((bf16[64,2,8,640]{3,2,1,0:T(8,128)(2,1)}), bf16[64,2,8,640]{3,2,1,0:T(8,128)(2,1)S(1)}, u32[]{:S(2)}, u32[]{:S(2)}) async-start(bf16[64,2,8,640]{3,2,1,0:T(8,128)(2,1)} %spatial.2), calls=%async_computation | async-start | bytes 2621440 | tf_op jit(solution)/shard_map/all_to_all | solution.py:479
  44.9 0.0 copy-done.5
  44.9 0.0 copy-done.6
  45.0 0.0 copy-done.7
  45.0 0.0 copy-done.8
  45.0 0.0 copy-done
  45.0 0.0 copy-done.1
  45.0 0.0 copy-done.2
  45.0 0.0 copy-done.3
  45.0 0.0 copy-start.4
  45.1 0.9 copy-done.4
  46.0 1.7 %prepare.1 = (bf16[1024,384]{1,0:T(8,128)(2,1)}, bf16[1024,384]{1,0:T(8,128)(2,1)}, bf16[384,1024]{1,0:T(8,128)(2,1)}, bf16[384,384]{1,0:T(8,128)(2,1)}) custom-call(bf16[3,320,320]{2,1,0:T(8,128)(2,1)S(1)} %copy-done, bf16[320,320]{1,0:T(8,128)(2,1)S(1)} %copy-done.1, bf16[320,320]{1,0:T(8,128)(2,1)S(1)} %copy-done.2, bf16[320,320]{1,0:T(8,128)(2,1)S(1)} %copy-done.3, ...), custom_call_target="tpu_custom_call" | custom-call | bytes 5000000 | tf_op jit(solution)/shard_map/prepare/pallas_call | solution.py:435
  47.7 8.8 %attend.3 = bf16[64,1,8,640]{3,2,1,0:T(8,128)(2,1)} custom-call(bf16[64,1,8,640]{3,2,1,0:T(8,128)(2,1)S(1)} %all-to-all-done.2.x_ref, bf16[1024,384]{1,0:T(8,128)(2,1)} %get-tuple-element.9.we_hbm, bf16[1024,384]{1,0:T(8,128)(2,1)} %get-tuple-element.10.wo_hbm, f32[8,384]{1,0:T(8,128)S(1)} %select_maximum_fusion.vector_ref, ...), custom_call_target="tpu_custom_call" | custom-call | flops 4000000000 | bytes 4000000 | tf_op jit(solution)/shard_map/attend/pallas_call | solution.py:327
  56.5 19.4 %all-to-all-done.x_ref = bf16[64,2,8,640]{3,2,1,0:T(8,128)(2,1)S(1)} async-done(((bf16[64,2,8,640]{3,2,1,0:T(8,128)(2,1)}), bf16[64,2,8,640]{3,2,1,0:T(8,128)(2,1)S(1)}, u32[]{:S(2)}, u32[]{:S(2)}) %all-to-all-start) | async-done | bytes 1310752 | tf_op jit(solution)/shard_map/all_to_all | solution.py:479
  75.9 5.2 %all-to-all-start.3 = ((bf16[64,1,8,640]{3,2,1,0:T(8,128)(2,1)}), bf16[64,1,8,640]{3,2,1,0:T(8,128)(2,1)S(1)}, u32[]{:S(2)}, u32[]{:S(2)}) async-start(bf16[64,1,8,640]{3,2,1,0:T(8,128)(2,1)} %attend.3), calls=%async_computation.3 | async-start | bytes 1310720 | tf_op jit(solution)/shard_map/all_to_all | solution.py:479
  81.2 15.8 %attend.2 = bf16[64,2,8,640]{3,2,1,0:T(8,128)(2,1)} custom-call(bf16[64,2,8,640]{3,2,1,0:T(8,128)(2,1)S(1)} %all-to-all-done.x_ref, bf16[1024,384]{1,0:T(8,128)(2,1)} %get-tuple-element.9.we_hbm, bf16[1024,384]{1,0:T(8,128)(2,1)} %get-tuple-element.10.wo_hbm, f32[8,384]{1,0:T(8,128)S(1)} %select_maximum_fusion.vector_ref, ...), custom_call_target="tpu_custom_call" | custom-call | flops 8000000000 | bytes 8000000 | tf_op jit(solution)/shard_map/attend/pallas_call | solution.py:327
  97.0 3.8 %all-to-all-done.3.x_ref = bf16[64,1,8,640]{3,2,1,0:T(8,128)(2,1)S(1)} async-done(((bf16[64,1,8,640]{3,2,1,0:T(8,128)(2,1)}), bf16[64,1,8,640]{3,2,1,0:T(8,128)(2,1)S(1)}, u32[]{:S(2)}, u32[]{:S(2)}) %all-to-all-start.3) | async-done | bytes 655392 | tf_op jit(solution)/shard_map/all_to_all | solution.py:479
  100.8 5.8 %all-to-all-start.1 = ((bf16[64,2,8,640]{3,2,1,0:T(8,128)(2,1)}), bf16[64,2,8,640]{3,2,1,0:T(8,128)(2,1)S(1)}, u32[]{:S(2)}, u32[]{:S(2)}) async-start(bf16[64,2,8,640]{3,2,1,0:T(8,128)(2,1)} %attend.2), calls=%async_computation.1 | async-start | bytes 2621440 | tf_op jit(solution)/shard_map/all_to_all | solution.py:479
  106.6 1.1 final.2.rest_0_
  107.7 32.2 %all-to-all-done.1.x_ref = bf16[64,2,8,640]{3,2,1,0:T(8,128)(2,1)S(1)} async-done(((bf16[64,2,8,640]{3,2,1,0:T(8,128)(2,1)}), bf16[64,2,8,640]{3,2,1,0:T(8,128)(2,1)S(1)}, u32[]{:S(2)}, u32[]{:S(2)}) %all-to-all-start.1) | async-done | bytes 1310752 | tf_op jit(solution)/shard_map/all_to_all | solution.py:479
  139.9 1.4 %final.3 = bf16[2,12,320,128]{3,2,1,0:T(8,128)(2,1)} custom-call(bf16[64,2,8,640]{3,2,1,0:T(8,128)(2,1)S(1)} %all-to-all-done.1.x_ref, bf16[2,12,320,128]{3,2,1,0:T(8,128)(2,1)} %final.2.rest_0_), custom_call_target="tpu_custom_call", output_to_operand_aliasing={{}: (1, {})} | custom-call | bytes 2800000 | tf_op jit(solution)/shard_map/final/pallas_call | solution.py:379
  (5 shorter events, 0.0 us)
Async XLA Ops:
  6.3 32.0 %all-to-all-start.2 = ((bf16[64,1,8,640]{3,2,1,0:T(8,128)(2,1)}), bf16[64,1,8,640]{3,2,1,0:T(8,128)(2,1)S(1)}, u32[]{:S(2)}, u32[]{:S(2)}) async-start(bf16[64,1,8,640]{3,2,1,0:T(8,128)(2,1)} %spatial.3), calls=%async_computation.2 | async-start | bytes 1310720 | tf_op jit(solution)/shard_map/all_to_all | solution.py:479
  17.7 2.6 %collective-permute-start = (bf16[2,1,320,128]{3,2,1,0:T(8,128)(2,1)S(1)}, bf16[2,1,320,128]{3,2,1,0:T(8,128)(2,1)S(1)}, u32[]{:S(2)}, u32[]{:S(2)}) collective-permute-start(bf16[2,1,320,128]{3,2,1,0:T(8,128)(2,1)S(1)} %get-tuple-element.14), channel_id=1, source_target_pairs={{0,1},{1,2},{2,3},{4,5},{5,6},{6,7},{8,9},{9,10},{10,11},{12,13},{... | collective-permute-start | bytes 491528 | tf_op jit(solution)/shard_map/ppermute | solution.py:466
  19.0 8.0 %collective-permute-start.1 = (bf16[2,1,320,128]{3,2,1,0:T(8,128)(2,1)S(1)}, bf16[2,1,320,128]{3,2,1,0:T(8,128)(2,1)S(1)}, u32[]{:S(2)}, u32[]{:S(2)}) collective-permute-start(bf16[2,1,320,128]{3,2,1,0:T(8,128)(2,1)S(1)} %get-tuple-element.13), channel_id=1, source_target_pairs={{1,0},{2,1},{3,2},{5,4},{6,5},{7,6},{9,8},{10,9},{11,10},{13,12},{... | collective-permute-start | bytes 491528 | tf_op jit(solution)/shard_map/ppermute | solution.py:467
  35.1 9.8 %copy-start.5 = (f32[320]{0:T(512)S(1)}, f32[320]{0:T(512)}, u32[]{:S(2)}) copy-start(f32[320]{0:T(512)} %param.16) | copy-start | bytes 3844
  35.1 9.8 %copy-start.6 = (f32[320]{0:T(512)S(1)}, f32[320]{0:T(512)}, u32[]{:S(2)}) copy-start(f32[320]{0:T(512)} %param.17) | copy-start | bytes 3844
  35.1 9.9 %copy-start.7 = (f32[320]{0:T(512)S(1)}, f32[320]{0:T(512)}, u32[]{:S(2)}) copy-start(f32[320]{0:T(512)} %param.18) | copy-start | bytes 3844
  35.1 9.9 %copy-start.8 = (f32[320]{0:T(512)S(1)}, f32[320]{0:T(512)}, u32[]{:S(2)}) copy-start(f32[320]{0:T(512)} %param.23) | copy-start | bytes 3844
  35.1 9.9 %copy-start = (bf16[3,320,320]{2,1,0:T(8,128)(2,1)S(1)}, bf16[3,320,320]{2,1,0:T(8,128)(2,1)}, u32[]{:S(2)}) copy-start(bf16[3,320,320]{2,1,0:T(8,128)(2,1)} %wt_ref.1) | copy-start | bytes 1843204
  35.1 9.9 %copy-start.1 = (bf16[320,320]{1,0:T(8,128)(2,1)S(1)}, bf16[320,320]{1,0:T(8,128)(2,1)}, u32[]{:S(2)}) copy-start(bf16[320,320]{1,0:T(8,128)(2,1)} %wq_ref.1) | copy-start | bytes 614404
  35.2 9.9 %copy-start.2 = (bf16[320,320]{1,0:T(8,128)(2,1)S(1)}, bf16[320,320]{1,0:T(8,128)(2,1)}, u32[]{:S(2)}) copy-start(bf16[320,320]{1,0:T(8,128)(2,1)} %wk_ref.1) | copy-start | bytes 614404
  35.2 9.9 %copy-start.3 = (bf16[320,320]{1,0:T(8,128)(2,1)S(1)}, bf16[320,320]{1,0:T(8,128)(2,1)}, u32[]{:S(2)}) copy-start(bf16[320,320]{1,0:T(8,128)(2,1)} %wv_ref.1) | copy-start | bytes 614404
  38.3 37.6 %all-to-all-start = ((bf16[64,2,8,640]{3,2,1,0:T(8,128)(2,1)}), bf16[64,2,8,640]{3,2,1,0:T(8,128)(2,1)S(1)}, u32[]{:S(2)}, u32[]{:S(2)}) async-start(bf16[64,2,8,640]{3,2,1,0:T(8,128)(2,1)} %spatial.2), calls=%async_computation | async-start | bytes 2621440 | tf_op jit(solution)/shard_map/all_to_all | solution.py:479
  45.0 0.9 copy-start.4
  75.9 24.9 %all-to-all-start.3 = ((bf16[64,1,8,640]{3,2,1,0:T(8,128)(2,1)}), bf16[64,1,8,640]{3,2,1,0:T(8,128)(2,1)S(1)}, u32[]{:S(2)}, u32[]{:S(2)}) async-start(bf16[64,1,8,640]{3,2,1,0:T(8,128)(2,1)} %attend.3), calls=%async_computation.3 | async-start | bytes 1310720 | tf_op jit(solution)/shard_map/all_to_all | solution.py:479
  100.8 39.1 %all-to-all-start.1 = ((bf16[64,2,8,640]{3,2,1,0:T(8,128)(2,1)}), bf16[64,2,8,640]{3,2,1,0:T(8,128)(2,1)S(1)}, u32[]{:S(2)}, u32[]{:S(2)}) async-start(bf16[64,2,8,640]{3,2,1,0:T(8,128)(2,1)} %attend.2), calls=%async_computation.1 | async-start | bytes 2621440 | tf_op jit(solution)/shard_map/all_to_all | solution.py:479

commit v3 on v2

--- a/solution.py
+++ b/solution.py
@@ -33,9 +33,10 @@
     return jnp.where(row == edge, 0.0, turned)
 
 
-def conv_kernel(parts, rows, w_hbm, b_ref, x_hbm, low_hbm, high_hbm, out, *scratch):
+def conv_kernel(parts, rows, w_hbm, b_hbm, x_hbm, low_hbm, high_hbm, out_hbm, *scratch):
     count = len(parts)
-    strips, turned, w_ref, w_even, w_odd, x_sem, w_sem = scratch
+    strips, turned, w_ref, w_even, w_odd, b_ref, out, x_sem, w_sem, o_sem = scratch
+    stores = []
     loads = []
     for h, chunk in enumerate(parts):
         first, last = chunk * CHUNK - 1, (chunk + 1) * CHUNK
@@ -54,6 +55,7 @@
                     )
                 )
     w_loads = [pltpu.make_async_copy(w_hbm.at[a], w_ref.at[a], w_sem.at[a]) for a in range(3)]
+    w_loads.append(pltpu.make_async_copy(b_hbm, b_ref, w_sem.at[3]))
     for load in loads + w_loads:
         load.start()
     for load in loads:
@@ -76,7 +78,10 @@
         w_even[at : at + C, 768:1024] = rest_w
         w_odd[64 + at : 64 + at + C, 768:1024] = rest_w
     lane = lax.broadcasted_iota(jnp.int32, (128, 128), 1)
-    rim_bias = jnp.concatenate([b_ref[0:1, 256:C], jnp.zeros((1, 64), F32)], axis=1)
+    w_loads[3].wait()
+    bias = b_ref[...].reshape(1, C)
+    main_bias = bias[:, 0:256]
+    rim_bias = jnp.concatenate([bias[:, 256:C], jnp.zeros((1, 64), F32)], axis=1)
     for h in range(count):
         for odd, weights in ((0, w_even), (1, w_odd)):
             starts = (0, 640) if odd == 0 else (256, 896)
@@ -94,7 +99,7 @@
                         shift_rows(part[:, 0:256], 1)
                         + part[:, 256:512]
                         + shift_rows(part[:, 512:768], -1)
-                        + b_ref[0:1, 0:256]
+                        + main_bias
                     )
                     out[to, h, :, f * 256 : (f + 1) * 256] = main.reshape(16, 8, 256).astype(BF)
                     pair = part[:, 768:896]
@@ -106,6 +111,13 @@
                     )
                 tail = jnp.where(lane < 64, tails[0], pltpu.roll(tails[1], 64, 1))
                 out[to, h, :, 512:640] = tail.reshape(16, 8, 128).astype(BF)
+                store = pltpu.make_async_copy(
+                    out.at[to, h], out_hbm.at[to, h], o_sem.at[len(stores)]
+                )
+                store.start()
+                stores.append(store)
+    for store in stores:
+        store.wait()
 
 
 def spatial_chunk(parts, low, x, high, w, b):
@@ -119,18 +131,21 @@
         high = x
     return pl.pallas_call(
         functools.partial(conv_kernel, parts, rows),
-        out_shape=jax.ShapeDtypeStruct(shape, BF),
+        out_shape=pltpu.HBM(shape, BF),
         grid=(1,),
-        in_specs=[far, full((1, C)), far, far, far],
-        out_specs=full(shape),
+        in_specs=[far, far, far, far, far],
+        out_specs=far,
         scratch_shapes=[
             pltpu.VMEM((count, 2, CHUNK + 2, C, 128), BF),
             pltpu.VMEM((count, 2, 128, (CHUNK + 2) * C), BF),
             pltpu.VMEM((3, 3, C, C), BF),
             pltpu.VMEM((1024, 1024), BF),
             pltpu.VMEM((1024, 1024), BF),
+            pltpu.VMEM((C,), F32),
+            pltpu.VMEM(shape, BF),
             pltpu.SemaphoreType.DMA((4 * count,)),
-            pltpu.SemaphoreType.DMA((3,)),
+            pltpu.SemaphoreType.DMA((4,)),
+            pltpu.SemaphoreType.DMA((4 * count,)),
         ],
         compiler_params=pltpu.CompilerParams(vmem_limit_bytes=32 << 20),
         cost_estimate=pl.CostEstimate(
@@ -359,7 +374,7 @@
 
 def final_kernel(x_ref, *rest):
     out = rest[-1]
-    for i in range(CHUNK):
+    for i in range(2):
         y = x_ref[i * 16 : (i + 1) * 16, 0].reshape(128, LANES).T
         out[0, i, 0:256, :] = y[0:256]
         out[1, i, 0:256, :] = y[256:512]
@@ -370,7 +385,7 @@
 def final_chunk(x, held, first, step, rows):
     count = x.shape[1]
     operands = [x]
-    specs = [pl.BlockSpec((64, 1, 8, LANES), lambda i: (0, i, 0, 0))]
+    specs = [pl.BlockSpec((32, 1, 8, LANES), lambda i: (i % 2, i // 2, 0, 0))]
     aliases = {}
     if held is not None:
         operands.append(held)
@@ -379,9 +394,11 @@
     return pl.pallas_call(
         final_kernel,
         out_shape=jax.ShapeDtypeStruct((2, rows, C, 128), BF),
-        grid=(count,),
+        grid=(2 * count,),
         in_specs=specs,
-        out_specs=pl.BlockSpec((2, CHUNK, C, 128), lambda i: (0, first + i * step, 0, 0)),
+        out_specs=pl.BlockSpec(
+            (2, 2, C, 128), lambda i: (0, 2 * (first + i // 2 * step) + i % 2, 0, 0)
+        ),
         input_output_aliases=aliases,
         compiler_params=pltpu.CompilerParams(vmem_limit_bytes=16 << 20),
         cost_estimate=pl.CostEstimate(
@@ -467,7 +484,7 @@
     high = lax.ppermute(x[:, :1], "row", backward)
     x = pltpu.with_memory_space_constraint(x, pltpu.HBM)
     w_spatial = pltpu.with_memory_space_constraint(w_spatial, pltpu.HBM)
-    bias = b_spatial.reshape(1, C)
+    bias = pltpu.with_memory_space_constraint(b_spatial, pltpu.HBM)
     w_even, w_odd, w_qkv, w_mix = prepared(w_temporal, w_query, w_key, w_value, w_out)
     vectors = jnp.pad(jnp.stack([b_temporal, ln_gain, ln_bias, b_out]), ((0, 4), (0, CP - C)))
     w_even, w_odd, w_qkv, w_mix = (

time: 144 us -> 144 us (level)
  no operation moved by 1% of the time
where the time goes in v3:
time: 144 us; the launch traced here: 141 us
  waiting for transfers between devices  65.4 us (45%)
  Pallas kernels  43.1 us (30%)
  starting transfers between devices  30.5 us (21%)
  local copies, waits for them, and re-layouts  2.03 us (1%)
    all_to_all x4, waiting for transfers between devices, exchange(): lax.all_to_all(value, 'frame', split_axis=0, concat_axis=0, tiled=True, a...  58.7 us
    all_to_all x4, starting transfers between devices, exchange(): lax.all_to_all(value, 'frame', split_axis=0, concat_axis=0, tiled=True, a...  27.9 us
    pallas_call x2, Pallas kernels, attend_chunk(): pl.pallas_call(attend_kernel, out_shape=jax.ShapeDtypeStruct(x.shape, BF)...  24.7 us
    pallas_call x2, Pallas kernels, spatial_chunk(): pl.pallas_call(functools.partial(conv_kernel, parts, rows), out_shape=plt...  13.7 us
    ppermute x1, waiting for transfers between devices, on_device(): high = lax.ppermute(x[:, :1], 'row', backward)  6.7 us
    pallas_call x2, Pallas kernels, final_chunk(): pl.pallas_call(final_kernel, out_shape=jax.ShapeDtypeStruct((2, rows, C,...  3.11 us
  transfers between devices with their start and end apart: 6, of which 5 were waited for; matrix products, arithmetic and copies ran while one was open for 1% of the time, Pallas kernels for 25%

profile of v3, /device:TPU:4, one launch (start us, length us, event | category | flops | bytes accessed | tf_op | source)
XLA Modules:
  0.0 141.3 jit_solution(6436748065606537837)
XLA Ops:
  0.0 5.8 %spatial.3 = bf16[64,1,8,640]{3,2,1,0:T(8,128)(2,1)} custom-call(bf16[3,3,320,320]{3,2,1,0:T(8,128)(2,1)} %w_hbm.3, f32[320]{0:T(512)} %b_hbm.3, bf16[2,12,320,128]{3,2,1,0:T(8,128)(2,1)} %bitcast.2, bf16[2,12,320,128]{3,2,1,0:T(8,128)(2,1)} %bitcast.3, bf16[2,12,320,128]{3,2,1,0:T(8,128)(2,1)} %bitcast.4), custom_call_target="tpu_custom_call" | custom-call | flops 2200000000 | bytes 4000000 | tf_op jit(solution)/shard_map/spatial/pallas_call | solution.py:132
  5.8 10.4 %all-to-all-start.2 = ((bf16[64,1,8,640]{3,2,1,0:T(8,128)(2,1)}), bf16[64,1,8,640]{3,2,1,0:T(8,128)(2,1)S(1)}, u32[]{:S(2)}, u32[]{:S(2)}) async-start(bf16[64,1,8,640]{3,2,1,0:T(8,128)(2,1)} %spatial.3), calls=%async_computation.2 | async-start | bytes 1310720 | tf_op jit(solution)/shard_map/all_to_all | solution.py:496
  16.2 1.0 fusion
  17.3 1.3 collective-permute-start
  18.6 1.3 collective-permute-start.1
  19.9 0.0 collective-permute-done.low_hbm
  19.9 6.7 %collective-permute-done.1.high_hbm = bf16[2,1,320,128]{3,2,1,0:T(8,128)(2,1)S(1)} collective-permute-done((bf16[2,1,320,128]{3,2,1,0:T(8,128)(2,1)S(1)}, bf16[2,1,320,128]{3,2,1,0:T(8,128)(2,1)S(1)}, u32[]{:S(2)}, u32[]{:S(2)}) %collective-permute-start.1) | collective-permute-done | bytes 163872 | tf_op jit(solution)/shard_map/ppermute | solution.py:484
  26.6 7.9 %spatial.2 = bf16[64,2,8,640]{3,2,1,0:T(8,128)(2,1)} custom-call(bf16[3,3,320,320]{3,2,1,0:T(8,128)(2,1)} %w_hbm.3, f32[320]{0:T(512)} %b_hbm.3, bf16[2,12,320,128]{3,2,1,0:T(8,128)(2,1)} %bitcast.6, bf16[2,1,320,128]{3,2,1,0:T(8,128)(2,1)S(1)} %collective-permute-done.low_hbm, bf16[2,1,320,128]{3,2,1,0:T(8,128)(2,1)S(1)} %collective-permute-done.1.high_hbm), custom_call_target="tpu_custom_call" | custom-call | flops 4400000000 | bytes 8000000 | tf_op jit(solution)/shard_map/spatial/pallas_call | solution.py:132
  34.5 0.0 copy-start.5
  34.5 0.0 copy-start.6
  34.5 0.0 copy-start.7
  34.5 0.0 copy-start.8
  34.5 0.0 copy-start
  34.5 0.0 copy-start.1
  34.5 0.0 copy-start.2
  34.6 0.0 copy-start.3
  34.6 3.3 %all-to-all-done.2.x_ref = bf16[64,1,8,640]{3,2,1,0:T(8,128)(2,1)S(1)} async-done(((bf16[64,1,8,640]{3,2,1,0:T(8,128)(2,1)}), bf16[64,1,8,640]{3,2,1,0:T(8,128)(2,1)S(1)}, u32[]{:S(2)}, u32[]{:S(2)}) %all-to-all-start.2) | async-done | bytes 655392 | tf_op jit(solution)/shard_map/all_to_all | solution.py:496
  37.8 6.5 %all-to-all-start = ((bf16[64,2,8,640]{3,2,1,0:T(8,128)(2,1)}), bf16[64,2,8,640]{3,2,1,0:T(8,128)(2,1)S(1)}, u32[]{:S(2)}, u32[]{:S(2)}) async-start(bf16[64,2,8,640]{3,2,1,0:T(8,128)(2,1)} %spatial.2), calls=%async_computation | async-start | bytes 2621440 | tf_op jit(solution)/shard_map/all_to_all | solution.py:496
  44.3 0.0 copy-done.5
  44.3 0.0 copy-done.6
  44.3 0.0 copy-done.7
  44.4 0.0 copy-done.8
  44.4 0.0 copy-done
  44.4 0.0 copy-done.1
  44.4 0.0 copy-done.2
  44.4 0.0 copy-done.3
  44.4 0.0 copy-start.4
  44.4 0.9 copy-done.4
  45.4 1.7 %prepare.1 = (bf16[1024,384]{1,0:T(8,128)(2,1)}, bf16[1024,384]{1,0:T(8,128)(2,1)}, bf16[384,1024]{1,0:T(8,128)(2,1)}, bf16[384,384]{1,0:T(8,128)(2,1)}) custom-call(bf16[3,320,320]{2,1,0:T(8,128)(2,1)S(1)} %copy-done, bf16[320,320]{1,0:T(8,128)(2,1)S(1)} %copy-done.1, bf16[320,320]{1,0:T(8,128)(2,1)S(1)} %copy-done.2, bf16[320,320]{1,0:T(8,128)(2,1)S(1)} %copy-done.3, ...), custom_call_target="tpu_custom_call" | custom-call | bytes 5000000 | tf_op jit(solution)/shard_map/prepare/pallas_call | solution.py:452
  47.1 8.8 %attend.3 = bf16[64,1,8,640]{3,2,1,0:T(8,128)(2,1)} custom-call(bf16[64,1,8,640]{3,2,1,0:T(8,128)(2,1)S(1)} %all-to-all-done.2.x_ref, bf16[1024,384]{1,0:T(8,128)(2,1)} %get-tuple-element.9.we_hbm, bf16[1024,384]{1,0:T(8,128)(2,1)} %get-tuple-element.10.wo_hbm, f32[8,384]{1,0:T(8,128)S(1)} %select_maximum_fusion.vector_ref, ...), custom_call_target="tpu_custom_call" | custom-call | flops 4000000000 | bytes 4000000 | tf_op jit(solution)/shard_map/attend/pallas_call | solution.py:342
  55.9 19.4 %all-to-all-done.x_ref = bf16[64,2,8,640]{3,2,1,0:T(8,128)(2,1)S(1)} async-done(((bf16[64,2,8,640]{3,2,1,0:T(8,128)(2,1)}), bf16[64,2,8,640]{3,2,1,0:T(8,128)(2,1)S(1)}, u32[]{:S(2)}, u32[]{:S(2)}) %all-to-all-start) | async-done | bytes 1310752 | tf_op jit(solution)/shard_map/all_to_all | solution.py:496
  75.3 5.2 %all-to-all-start.3 = ((bf16[64,1,8,640]{3,2,1,0:T(8,128)(2,1)}), bf16[64,1,8,640]{3,2,1,0:T(8,128)(2,1)S(1)}, u32[]{:S(2)}, u32[]{:S(2)}) async-start(bf16[64,1,8,640]{3,2,1,0:T(8,128)(2,1)} %attend.3), calls=%async_computation.3 | async-start | bytes 1310720 | tf_op jit(solution)/shard_map/all_to_all | solution.py:496
  80.5 15.8 %attend.2 = bf16[64,2,8,640]{3,2,1,0:T(8,128)(2,1)} custom-call(bf16[64,2,8,640]{3,2,1,0:T(8,128)(2,1)S(1)} %all-to-all-done.x_ref, bf16[1024,384]{1,0:T(8,128)(2,1)} %get-tuple-element.9.we_hbm, bf16[1024,384]{1,0:T(8,128)(2,1)} %get-tuple-element.10.wo_hbm, f32[8,384]{1,0:T(8,128)S(1)} %select_maximum_fusion.vector_ref, ...), custom_call_target="tpu_custom_call" | custom-call | flops 8000000000 | bytes 8000000 | tf_op jit(solution)/shard_map/attend/pallas_call | solution.py:342
  96.4 3.8 %all-to-all-done.3.x_ref = bf16[64,1,8,640]{3,2,1,0:T(8,128)(2,1)S(1)} async-done(((bf16[64,1,8,640]{3,2,1,0:T(8,128)(2,1)}), bf16[64,1,8,640]{3,2,1,0:T(8,128)(2,1)S(1)}, u32[]{:S(2)}, u32[]{:S(2)}) %all-to-all-start.3) | async-done | bytes 655392 | tf_op jit(solution)/shard_map/all_to_all | solution.py:496
  100.2 5.8 %all-to-all-start.1 = ((bf16[64,2,8,640]{3,2,1,0:T(8,128)(2,1)}), bf16[64,2,8,640]{3,2,1,0:T(8,128)(2,1)S(1)}, u32[]{:S(2)}, u32[]{:S(2)}) async-start(bf16[64,2,8,640]{3,2,1,0:T(8,128)(2,1)} %attend.2), calls=%async_computation.1 | async-start | bytes 2621440 | tf_op jit(solution)/shard_map/all_to_all | solution.py:496
  106.0 1.1 final.2.rest_0_
  107.1 32.2 %all-to-all-done.1.x_ref = bf16[64,2,8,640]{3,2,1,0:T(8,128)(2,1)S(1)} async-done(((bf16[64,2,8,640]{3,2,1,0:T(8,128)(2,1)}), bf16[64,2,8,640]{3,2,1,0:T(8,128)(2,1)S(1)}, u32[]{:S(2)}, u32[]{:S(2)}) %all-to-all-start.1) | async-done | bytes 1310752 | tf_op jit(solution)/shard_map/all_to_all | solution.py:496
  139.3 2.0 %final.3 = bf16[2,12,320,128]{3,2,1,0:T(8,128)(2,1)} custom-call(bf16[64,2,8,640]{3,2,1,0:T(8,128)(2,1)S(1)} %all-to-all-done.1.x_ref, bf16[2,12,320,128]{3,2,1,0:T(8,128)(2,1)} %final.2.rest_0_), custom_call_target="tpu_custom_call", output_to_operand_aliasing={{}: (1, {})} | custom-call | bytes 2800000 | tf_op jit(solution)/shard_map/final/pallas_call | solution.py:394
  (5 shorter events, 0.0 us)
Async XLA Ops:
  5.8 32.0 %all-to-all-start.2 = ((bf16[64,1,8,640]{3,2,1,0:T(8,128)(2,1)}), bf16[64,1,8,640]{3,2,1,0:T(8,128)(2,1)S(1)}, u32[]{:S(2)}, u32[]{:S(2)}) async-start(bf16[64,1,8,640]{3,2,1,0:T(8,128)(2,1)} %spatial.3), calls=%async_computation.2 | async-start | bytes 1310720 | tf_op jit(solution)/shard_map/all_to_all | solution.py:496
  17.3 2.6 %collective-permute-start = (bf16[2,1,320,128]{3,2,1,0:T(8,128)(2,1)S(1)}, bf16[2,1,320,128]{3,2,1,0:T(8,128)(2,1)S(1)}, u32[]{:S(2)}, u32[]{:S(2)}) collective-permute-start(bf16[2,1,320,128]{3,2,1,0:T(8,128)(2,1)S(1)} %get-tuple-element.14), channel_id=1, source_target_pairs={{0,1},{1,2},{2,3},{4,5},{5,6},{6,7},{8,9},{9,10},{10,11},{12,13},{... | collective-permute-start | bytes 491528 | tf_op jit(solution)/shard_map/ppermute | solution.py:483
  18.6 8.0 %collective-permute-start.1 = (bf16[2,1,320,128]{3,2,1,0:T(8,128)(2,1)S(1)}, bf16[2,1,320,128]{3,2,1,0:T(8,128)(2,1)S(1)}, u32[]{:S(2)}, u32[]{:S(2)}) collective-permute-start(bf16[2,1,320,128]{3,2,1,0:T(8,128)(2,1)S(1)} %get-tuple-element.13), channel_id=1, source_target_pairs={{1,0},{2,1},{3,2},{5,4},{6,5},{7,6},{9,8},{10,9},{11,10},{13,12},{... | collective-permute-start | bytes 491528 | tf_op jit(solution)/shard_map/ppermute | solution.py:484
  34.5 9.8 %copy-start.5 = (f32[320]{0:T(512)S(1)}, f32[320]{0:T(512)}, u32[]{:S(2)}) copy-start(f32[320]{0:T(512)} %param.16) | copy-start | bytes 3844
  34.5 9.8 %copy-start.6 = (f32[320]{0:T(512)S(1)}, f32[320]{0:T(512)}, u32[]{:S(2)}) copy-start(f32[320]{0:T(512)} %param.17) | copy-start | bytes 3844
  34.5 9.9 %copy-start.7 = (f32[320]{0:T(512)S(1)}, f32[320]{0:T(512)}, u32[]{:S(2)}) copy-start(f32[320]{0:T(512)} %param.18) | copy-start | bytes 3844
  34.5 9.9 %copy-start.8 = (f32[320]{0:T(512)S(1)}, f32[320]{0:T(512)}, u32[]{:S(2)}) copy-start(f32[320]{0:T(512)} %param.23) | copy-start | bytes 3844
  34.5 9.9 %copy-start = (bf16[3,320,320]{2,1,0:T(8,128)(2,1)S(1)}, bf16[3,320,320]{2,1,0:T(8,128)(2,1)}, u32[]{:S(2)}) copy-start(bf16[3,320,320]{2,1,0:T(8,128)(2,1)} %wt_ref.1) | copy-start | bytes 1843204
  34.5 9.9 %copy-start.1 = (bf16[320,320]{1,0:T(8,128)(2,1)S(1)}, bf16[320,320]{1,0:T(8,128)(2,1)}, u32[]{:S(2)}) copy-start(bf16[320,320]{1,0:T(8,128)(2,1)} %wq_ref.1) | copy-start | bytes 614404
  34.5 9.9 %copy-start.2 = (bf16[320,320]{1,0:T(8,128)(2,1)S(1)}, bf16[320,320]{1,0:T(8,128)(2,1)}, u32[]{:S(2)}) copy-start(bf16[320,320]{1,0:T(8,128)(2,1)} %wk_ref.1) | copy-start | bytes 614404
  34.6 9.9 %copy-start.3 = (bf16[320,320]{1,0:T(8,128)(2,1)S(1)}, bf16[320,320]{1,0:T(8,128)(2,1)}, u32[]{:S(2)}) copy-start(bf16[320,320]{1,0:T(8,128)(2,1)} %wv_ref.1) | copy-start | bytes 614404
  37.8 37.5 %all-to-all-start = ((bf16[64,2,8,640]{3,2,1,0:T(8,128)(2,1)}), bf16[64,2,8,640]{3,2,1,0:T(8,128)(2,1)S(1)}, u32[]{:S(2)}, u32[]{:S(2)}) async-start(bf16[64,2,8,640]{3,2,1,0:T(8,128)(2,1)} %spatial.2), calls=%async_computation | async-start | bytes 2621440 | tf_op jit(solution)/shard_map/all_to_all | solution.py:496
  44.4 0.9 copy-start.4
  75.3 24.9 %all-to-all-start.3 = ((bf16[64,1,8,640]{3,2,1,0:T(8,128)(2,1)}), bf16[64,1,8,640]{3,2,1,0:T(8,128)(2,1)S(1)}, u32[]{:S(2)}, u32[]{:S(2)}) async-start(bf16[64,1,8,640]{3,2,1,0:T(8,128)(2,1)} %attend.3), calls=%async_computation.3 | async-start | bytes 1310720 | tf_op jit(solution)/shard_map/all_to_all | solution.py:496
  100.2 39.1 %all-to-all-start.1 = ((bf16[64,2,8,640]{3,2,1,0:T(8,128)(2,1)}), bf16[64,2,8,640]{3,2,1,0:T(8,128)(2,1)S(1)}, u32[]{:S(2)}, u32[]{:S(2)}) async-start(bf16[64,2,8,640]{3,2,1,0:T(8,128)(2,1)} %attend.2), calls=%async_computation.1 | async-start | bytes 2621440 | tf_op jit(solution)/shard_map/all_to_all | solution.py:496

commit v4 on v3

--- a/solution.py
+++ b/solution.py
@@ -374,7 +374,7 @@
 
 def final_kernel(x_ref, *rest):
     out = rest[-1]
-    for i in range(2):
+    for i in range(CHUNK):
         y = x_ref[i * 16 : (i + 1) * 16, 0].reshape(128, LANES).T
         out[0, i, 0:256, :] = y[0:256]
         out[1, i, 0:256, :] = y[256:512]
@@ -385,7 +385,7 @@
 def final_chunk(x, held, first, step, rows):
     count = x.shape[1]
     operands = [x]
-    specs = [pl.BlockSpec((32, 1, 8, LANES), lambda i: (i % 2, i // 2, 0, 0))]
+    specs = [pl.BlockSpec((64, 1, 8, LANES), lambda i: (0, i, 0, 0))]
     aliases = {}
     if held is not None:
         operands.append(held)
@@ -394,11 +394,9 @@
     return pl.pallas_call(
         final_kernel,
         out_shape=jax.ShapeDtypeStruct((2, rows, C, 128), BF),
-        grid=(2 * count,),
+        grid=(count,),
         in_specs=specs,
-        out_specs=pl.BlockSpec(
-            (2, 2, C, 128), lambda i: (0, 2 * (first + i // 2 * step) + i % 2, 0, 0)
-        ),
+        out_specs=pl.BlockSpec((2, CHUNK, C, 128), lambda i: (0, first + i * step, 0, 0)),
         input_output_aliases=aliases,
         compiler_params=pltpu.CompilerParams(vmem_limit_bytes=16 << 20),
         cost_estimate=pl.CostEstimate(

time: 144 us -> 143 us (level)
  no operation moved by 1% of the time
where the time goes in v4:
time: 143 us; the launch traced here: 141 us
  waiting for transfers between devices  65.4 us (46%)
  Pallas kernels  42.5 us (30%)
  starting transfers between devices  30.5 us (21%)
  local copies, waits for them, and re-layouts  2.03 us (1%)
    all_to_all x4, waiting for transfers between devices, exchange(): lax.all_to_all(value, 'frame', split_axis=0, concat_axis=0, tiled=True, a...  58.7 us
    all_to_all x4, starting transfers between devices, exchange(): lax.all_to_all(value, 'frame', split_axis=0, concat_axis=0, tiled=True, a...  27.9 us
    pallas_call x2, Pallas kernels, attend_chunk(): pl.pallas_call(attend_kernel, out_shape=jax.ShapeDtypeStruct(x.shape, BF)...  24.7 us
    pallas_call x2, Pallas kernels, spatial_chunk(): pl.pallas_call(functools.partial(conv_kernel, parts, rows), out_shape=plt...  13.7 us
    ppermute x1, waiting for transfers between devices, on_device(): high = lax.ppermute(x[:, :1], 'row', backward)  6.7 us
  transfers between devices with their start and end apart: 6, of which 5 were waited for; matrix products, arithmetic and copies ran while one was open for 1% of the time, Pallas kernels for 25%

profile of v4, /device:TPU:4, one launch (start us, length us, event | category | flops | bytes accessed | tf_op | source)
XLA Modules:
  0.0 140.7 jit_solution(3314956440098330774)
XLA Ops:
  0.0 5.8 %spatial.3 = bf16[64,1,8,640]{3,2,1,0:T(8,128)(2,1)} custom-call(bf16[3,3,320,320]{3,2,1,0:T(8,128)(2,1)} %w_hbm.3, f32[320]{0:T(512)} %b_hbm.3, bf16[2,12,320,128]{3,2,1,0:T(8,128)(2,1)} %bitcast.2, bf16[2,12,320,128]{3,2,1,0:T(8,128)(2,1)} %bitcast.3, bf16[2,12,320,128]{3,2,1,0:T(8,128)(2,1)} %bitcast.4), custom_call_target="tpu_custom_call" | custom-call | flops 2200000000 | bytes 4000000 | tf_op jit(solution)/shard_map/spatial/pallas_call | solution.py:132
  5.8 10.4 %all-to-all-start.2 = ((bf16[64,1,8,640]{3,2,1,0:T(8,128)(2,1)}), bf16[64,1,8,640]{3,2,1,0:T(8,128)(2,1)S(1)}, u32[]{:S(2)}, u32[]{:S(2)}) async-start(bf16[64,1,8,640]{3,2,1,0:T(8,128)(2,1)} %spatial.3), calls=%async_computation.2 | async-start | bytes 1310720 | tf_op jit(solution)/shard_map/all_to_all | solution.py:494
  16.2 1.0 fusion
  17.3 1.3 collective-permute-start
  18.6 1.3 collective-permute-start.1
  19.9 0.0 collective-permute-done.low_hbm
  19.9 6.7 %collective-permute-done.1.high_hbm = bf16[2,1,320,128]{3,2,1,0:T(8,128)(2,1)S(1)} collective-permute-done((bf16[2,1,320,128]{3,2,1,0:T(8,128)(2,1)S(1)}, bf16[2,1,320,128]{3,2,1,0:T(8,128)(2,1)S(1)}, u32[]{:S(2)}, u32[]{:S(2)}) %collective-permute-start.1) | collective-permute-done | bytes 163872 | tf_op jit(solution)/shard_map/ppermute | solution.py:482
  26.6 7.9 %spatial.2 = bf16[64,2,8,640]{3,2,1,0:T(8,128)(2,1)} custom-call(bf16[3,3,320,320]{3,2,1,0:T(8,128)(2,1)} %w_hbm.3, f32[320]{0:T(512)} %b_hbm.3, bf16[2,12,320,128]{3,2,1,0:T(8,128)(2,1)} %bitcast.6, bf16[2,1,320,128]{3,2,1,0:T(8,128)(2,1)S(1)} %collective-permute-done.low_hbm, bf16[2,1,320,128]{3,2,1,0:T(8,128)(2,1)S(1)} %collective-permute-done.1.high_hbm), custom_call_target="tpu_custom_call" | custom-call | flops 4400000000 | bytes 8000000 | tf_op jit(solution)/shard_map/spatial/pallas_call | solution.py:132
  34.5 0.0 copy-start.5
  34.5 0.0 copy-start.6
  34.5 0.0 copy-start.7
  34.5 0.0 copy-start.8
  34.5 0.0 copy-start
  34.5 0.0 copy-start.1
  34.5 0.0 copy-start.2
  34.6 0.0 copy-start.3
  34.6 3.3 %all-to-all-done.2.x_ref = bf16[64,1,8,640]{3,2,1,0:T(8,128)(2,1)S(1)} async-done(((bf16[64,1,8,640]{3,2,1,0:T(8,128)(2,1)}), bf16[64,1,8,640]{3,2,1,0:T(8,128)(2,1)S(1)}, u32[]{:S(2)}, u32[]{:S(2)}) %all-to-all-start.2) | async-done | bytes 655392 | tf_op jit(solution)/shard_map/all_to_all | solution.py:494
  37.8 6.5 %all-to-all-start = ((bf16[64,2,8,640]{3,2,1,0:T(8,128)(2,1)}), bf16[64,2,8,640]{3,2,1,0:T(8,128)(2,1)S(1)}, u32[]{:S(2)}, u32[]{:S(2)}) async-start(bf16[64,2,8,640]{3,2,1,0:T(8,128)(2,1)} %spatial.2), calls=%async_computation | async-start | bytes 2621440 | tf_op jit(solution)/shard_map/all_to_all | solution.py:494
  44.3 0.0 copy-done.5
  44.3 0.0 copy-done.6
  44.3 0.0 copy-done.7
  44.4 0.0 copy-done.8
  44.4 0.0 copy-done
  44.4 0.0 copy-done.1
  44.4 0.0 copy-done.2
  44.4 0.0 copy-done.3
  44.4 0.0 copy-start.4
  44.4 0.9 copy-done.4
  45.4 1.7 %prepare.1 = (bf16[1024,384]{1,0:T(8,128)(2,1)}, bf16[1024,384]{1,0:T(8,128)(2,1)}, bf16[384,1024]{1,0:T(8,128)(2,1)}, bf16[384,384]{1,0:T(8,128)(2,1)}) custom-call(bf16[3,320,320]{2,1,0:T(8,128)(2,1)S(1)} %copy-done, bf16[320,320]{1,0:T(8,128)(2,1)S(1)} %copy-done.1, bf16[320,320]{1,0:T(8,128)(2,1)S(1)} %copy-done.2, bf16[320,320]{1,0:T(8,128)(2,1)S(1)} %copy-done.3, ...), custom_call_target="tpu_custom_call" | custom-call | bytes 5000000 | tf_op jit(solution)/shard_map/prepare/pallas_call | solution.py:450
  47.1 8.8 %attend.3 = bf16[64,1,8,640]{3,2,1,0:T(8,128)(2,1)} custom-call(bf16[64,1,8,640]{3,2,1,0:T(8,128)(2,1)S(1)} %all-to-all-done.2.x_ref, bf16[1024,384]{1,0:T(8,128)(2,1)} %get-tuple-element.9.we_hbm, bf16[1024,384]{1,0:T(8,128)(2,1)} %get-tuple-element.10.wo_hbm, f32[8,384]{1,0:T(8,128)S(1)} %select_maximum_fusion.vector_ref, ...), custom_call_target="tpu_custom_call" | custom-call | flops 4000000000 | bytes 4000000 | tf_op jit(solution)/shard_map/attend/pallas_call | solution.py:342
  55.9 19.4 %all-to-all-done.x_ref = bf16[64,2,8,640]{3,2,1,0:T(8,128)(2,1)S(1)} async-done(((bf16[64,2,8,640]{3,2,1,0:T(8,128)(2,1)}), bf16[64,2,8,640]{3,2,1,0:T(8,128)(2,1)S(1)}, u32[]{:S(2)}, u32[]{:S(2)}) %all-to-all-start) | async-done | bytes 1310752 | tf_op jit(solution)/shard_map/all_to_all | solution.py:494
  75.3 5.2 %all-to-all-start.3 = ((bf16[64,1,8,640]{3,2,1,0:T(8,128)(2,1)}), bf16[64,1,8,640]{3,2,1,0:T(8,128)(2,1)S(1)}, u32[]{:S(2)}, u32[]{:S(2)}) async-start(bf16[64,1,8,640]{3,2,1,0:T(8,128)(2,1)} %attend.3), calls=%async_computation.3 | async-start | bytes 1310720 | tf_op jit(solution)/shard_map/all_to_all | solution.py:494
  80.5 15.8 %attend.2 = bf16[64,2,8,640]{3,2,1,0:T(8,128)(2,1)} custom-call(bf16[64,2,8,640]{3,2,1,0:T(8,128)(2,1)S(1)} %all-to-all-done.x_ref, bf16[1024,384]{1,0:T(8,128)(2,1)} %get-tuple-element.9.we_hbm, bf16[1024,384]{1,0:T(8,128)(2,1)} %get-tuple-element.10.wo_hbm, f32[8,384]{1,0:T(8,128)S(1)} %select_maximum_fusion.vector_ref, ...), custom_call_target="tpu_custom_call" | custom-call | flops 8000000000 | bytes 8000000 | tf_op jit(solution)/shard_map/attend/pallas_call | solution.py:342
  96.4 3.8 %all-to-all-done.3.x_ref = bf16[64,1,8,640]{3,2,1,0:T(8,128)(2,1)S(1)} async-done(((bf16[64,1,8,640]{3,2,1,0:T(8,128)(2,1)}), bf16[64,1,8,640]{3,2,1,0:T(8,128)(2,1)S(1)}, u32[]{:S(2)}, u32[]{:S(2)}) %all-to-all-start.3) | async-done | bytes 655392 | tf_op jit(solution)/shard_map/all_to_all | solution.py:494
  100.2 5.8 %all-to-all-start.1 = ((bf16[64,2,8,640]{3,2,1,0:T(8,128)(2,1)}), bf16[64,2,8,640]{3,2,1,0:T(8,128)(2,1)S(1)}, u32[]{:S(2)}, u32[]{:S(2)}) async-start(bf16[64,2,8,640]{3,2,1,0:T(8,128)(2,1)} %attend.2), calls=%async_computation.1 | async-start | bytes 2621440 | tf_op jit(solution)/shard_map/all_to_all | solution.py:494
  106.0 1.1 final.2.rest_0_
  107.0 32.2 %all-to-all-done.1.x_ref = bf16[64,2,8,640]{3,2,1,0:T(8,128)(2,1)S(1)} async-done(((bf16[64,2,8,640]{3,2,1,0:T(8,128)(2,1)}), bf16[64,2,8,640]{3,2,1,0:T(8,128)(2,1)S(1)}, u32[]{:S(2)}, u32[]{:S(2)}) %all-to-all-start.1) | async-done | bytes 1310752 | tf_op jit(solution)/shard_map/all_to_all | solution.py:494
  139.3 1.4 %final.3 = bf16[2,12,320,128]{3,2,1,0:T(8,128)(2,1)} custom-call(bf16[64,2,8,640]{3,2,1,0:T(8,128)(2,1)S(1)} %all-to-all-done.1.x_ref, bf16[2,12,320,128]{3,2,1,0:T(8,128)(2,1)} %final.2.rest_0_), custom_call_target="tpu_custom_call", output_to_operand_aliasing={{}: (1, {})} | custom-call | bytes 2800000 | tf_op jit(solution)/shard_map/final/pallas_call | solution.py:394
  (5 shorter events, 0.0 us)
Async XLA Ops:
  5.8 32.0 %all-to-all-start.2 = ((bf16[64,1,8,640]{3,2,1,0:T(8,128)(2,1)}), bf16[64,1,8,640]{3,2,1,0:T(8,128)(2,1)S(1)}, u32[]{:S(2)}, u32[]{:S(2)}) async-start(bf16[64,1,8,640]{3,2,1,0:T(8,128)(2,1)} %spatial.3), calls=%async_computation.2 | async-start | bytes 1310720 | tf_op jit(solution)/shard_map/all_to_all | solution.py:494
  17.3 2.6 %collective-permute-start = (bf16[2,1,320,128]{3,2,1,0:T(8,128)(2,1)S(1)}, bf16[2,1,320,128]{3,2,1,0:T(8,128)(2,1)S(1)}, u32[]{:S(2)}, u32[]{:S(2)}) collective-permute-start(bf16[2,1,320,128]{3,2,1,0:T(8,128)(2,1)S(1)} %get-tuple-element.14), channel_id=1, source_target_pairs={{0,1},{1,2},{2,3},{4,5},{5,6},{6,7},{8,9},{9,10},{10,11},{12,13},{... | collective-permute-start | bytes 491528 | tf_op jit(solution)/shard_map/ppermute | solution.py:481
  18.6 8.0 %collective-permute-start.1 = (bf16[2,1,320,128]{3,2,1,0:T(8,128)(2,1)S(1)}, bf16[2,1,320,128]{3,2,1,0:T(8,128)(2,1)S(1)}, u32[]{:S(2)}, u32[]{:S(2)}) collective-permute-start(bf16[2,1,320,128]{3,2,1,0:T(8,128)(2,1)S(1)} %get-tuple-element.13), channel_id=1, source_target_pairs={{1,0},{2,1},{3,2},{5,4},{6,5},{7,6},{9,8},{10,9},{11,10},{13,12},{... | collective-permute-start | bytes 491528 | tf_op jit(solution)/shard_map/ppermute | solution.py:482
  34.5 9.8 %copy-start.5 = (f32[320]{0:T(512)S(1)}, f32[320]{0:T(512)}, u32[]{:S(2)}) copy-start(f32[320]{0:T(512)} %param.16) | copy-start | bytes 3844
  34.5 9.8 %copy-start.6 = (f32[320]{0:T(512)S(1)}, f32[320]{0:T(512)}, u32[]{:S(2)}) copy-start(f32[320]{0:T(512)} %param.17) | copy-start | bytes 3844
  34.5 9.9 %copy-start.7 = (f32[320]{0:T(512)S(1)}, f32[320]{0:T(512)}, u32[]{:S(2)}) copy-start(f32[320]{0:T(512)} %param.18) | copy-start | bytes 3844
  34.5 9.9 %copy-start.8 = (f32[320]{0:T(512)S(1)}, f32[320]{0:T(512)}, u32[]{:S(2)}) copy-start(f32[320]{0:T(512)} %param.23) | copy-start | bytes 3844
  34.5 9.9 %copy-start = (bf16[3,320,320]{2,1,0:T(8,128)(2,1)S(1)}, bf16[3,320,320]{2,1,0:T(8,128)(2,1)}, u32[]{:S(2)}) copy-start(bf16[3,320,320]{2,1,0:T(8,128)(2,1)} %wt_ref.1) | copy-start | bytes 1843204
  34.5 9.9 %copy-start.1 = (bf16[320,320]{1,0:T(8,128)(2,1)S(1)}, bf16[320,320]{1,0:T(8,128)(2,1)}, u32[]{:S(2)}) copy-start(bf16[320,320]{1,0:T(8,128)(2,1)} %wq_ref.1) | copy-start | bytes 614404
  34.5 9.9 %copy-start.2 = (bf16[320,320]{1,0:T(8,128)(2,1)S(1)}, bf16[320,320]{1,0:T(8,128)(2,1)}, u32[]{:S(2)}) copy-start(bf16[320,320]{1,0:T(8,128)(2,1)} %wk_ref.1) | copy-start | bytes 614404
  34.6 9.9 %copy-start.3 = (bf16[320,320]{1,0:T(8,128)(2,1)S(1)}, bf16[320,320]{1,0:T(8,128)(2,1)}, u32[]{:S(2)}) copy-start(bf16[320,320]{1,0:T(8,128)(2,1)} %wv_ref.1) | copy-start | bytes 614404
  37.8 37.5 %all-to-all-start = ((bf16[64,2,8,640]{3,2,1,0:T(8,128)(2,1)}), bf16[64,2,8,640]{3,2,1,0:T(8,128)(2,1)S(1)}, u32[]{:S(2)}, u32[]{:S(2)}) async-start(bf16[64,2,8,640]{3,2,1,0:T(8,128)(2,1)} %spatial.2), calls=%async_computation | async-start | bytes 2621440 | tf_op jit(solution)/shard_map/all_to_all | solution.py:494
  44.4 0.9 copy-start.4
  75.3 24.9 %all-to-all-start.3 = ((bf16[64,1,8,640]{3,2,1,0:T(8,128)(2,1)}), bf16[64,1,8,640]{3,2,1,0:T(8,128)(2,1)S(1)}, u32[]{:S(2)}, u32[]{:S(2)}) async-start(bf16[64,1,8,640]{3,2,1,0:T(8,128)(2,1)} %attend.3), calls=%async_computation.3 | async-start | bytes 1310720 | tf_op jit(solution)/shard_map/all_to_all | solution.py:494
  100.2 39.1 %all-to-all-start.1 = ((bf16[64,2,8,640]{3,2,1,0:T(8,128)(2,1)}), bf16[64,2,8,640]{3,2,1,0:T(8,128)(2,1)S(1)}, u32[]{:S(2)}, u32[]{:S(2)}) async-start(bf16[64,2,8,640]{3,2,1,0:T(8,128)(2,1)} %attend.2), calls=%async_computation.1 | async-start | bytes 2621440 | tf_op jit(solution)/shard_map/all_to_all | solution.py:494

commit v5 on v4

--- a/solution.py
+++ b/solution.py
@@ -374,8 +374,9 @@
 
 def final_kernel(x_ref, *rest):
     out = rest[-1]
+    step = pl.program_id(0)
     for i in range(CHUNK):
-        y = x_ref[i * 16 : (i + 1) * 16, 0].reshape(128, LANES).T
+        y = x_ref[i * 16 : (i + 1) * 16, step].reshape(128, LANES).T
         out[0, i, 0:256, :] = y[0:256]
         out[1, i, 0:256, :] = y[256:512]
         out[0, i, 256:320, :] = y[512:576]
@@ -385,7 +386,7 @@
 def final_chunk(x, held, first, step, rows):
     count = x.shape[1]
     operands = [x]
-    specs = [pl.BlockSpec((64, 1, 8, LANES), lambda i: (0, i, 0, 0))]
+    specs = [pl.BlockSpec(memory_space=pltpu.VMEM)]
     aliases = {}
     if held is not None:
         operands.append(held)

time: 143 us -> 143 us (level)
  no operation moved by 1% of the time
where the time goes in v5:
time: 143 us; the launch traced here: 141 us
  waiting for transfers between devices  65.4 us (46%)
  Pallas kernels  42.4 us (30%)
  starting transfers between devices  30.5 us (21%)
  local copies, waits for them, and re-layouts  2.03 us (1%)
    all_to_all x4, waiting for transfers between devices, exchange(): lax.all_to_all(value, 'frame', split_axis=0, concat_axis=0, tiled=True, a...  58.7 us
    all_to_all x4, starting transfers between devices, exchange(): lax.all_to_all(value, 'frame', split_axis=0, concat_axis=0, tiled=True, a...  27.9 us
    pallas_call x2, Pallas kernels, attend_chunk(): pl.pallas_call(attend_kernel, out_shape=jax.ShapeDtypeStruct(x.shape, BF)...  24.7 us
    pallas_call x2, Pallas kernels, spatial_chunk(): pl.pallas_call(functools.partial(conv_kernel, parts, rows), out_shape=plt...  13.7 us
    ppermute x1, waiting for transfers between devices, on_device(): high = lax.ppermute(x[:, :1], 'row', backward)  6.7 us
  transfers between devices with their start and end apart: 6, of which 5 were waited for; matrix products, arithmetic and copies ran while one was open for 1% of the time, Pallas kernels for 25%

profile of v5, /device:TPU:4, one launch (start us, length us, event | category | flops | bytes accessed | tf_op | source)
XLA Modules:
  0.0 140.6 jit_solution(8168901989713674708)
XLA Ops:
  0.0 5.8 %spatial.3 = bf16[64,1,8,640]{3,2,1,0:T(8,128)(2,1)} custom-call(bf16[3,3,320,320]{3,2,1,0:T(8,128)(2,1)} %w_hbm.3, f32[320]{0:T(512)} %b_hbm.3, bf16[2,12,320,128]{3,2,1,0:T(8,128)(2,1)} %bitcast.2, bf16[2,12,320,128]{3,2,1,0:T(8,128)(2,1)} %bitcast.3, bf16[2,12,320,128]{3,2,1,0:T(8,128)(2,1)} %bitcast.4), custom_call_target="tpu_custom_call" | custom-call | flops 2200000000 | bytes 4000000 | tf_op jit(solution)/shard_map/spatial/pallas_call | solution.py:132
  5.8 10.4 %all-to-all-start.2 = ((bf16[64,1,8,640]{3,2,1,0:T(8,128)(2,1)}), bf16[64,1,8,640]{3,2,1,0:T(8,128)(2,1)S(1)}, u32[]{:S(2)}, u32[]{:S(2)}) async-start(bf16[64,1,8,640]{3,2,1,0:T(8,128)(2,1)} %spatial.3), calls=%async_computation.2 | async-start | bytes 1310720 | tf_op jit(solution)/shard_map/all_to_all | solution.py:495
  16.2 1.0 fusion
  17.3 1.3 collective-permute-start
  18.6 1.3 collective-permute-start.1
  19.9 0.0 collective-permute-done.low_hbm
  19.9 6.7 %collective-permute-done.1.high_hbm = bf16[2,1,320,128]{3,2,1,0:T(8,128)(2,1)S(1)} collective-permute-done((bf16[2,1,320,128]{3,2,1,0:T(8,128)(2,1)S(1)}, bf16[2,1,320,128]{3,2,1,0:T(8,128)(2,1)S(1)}, u32[]{:S(2)}, u32[]{:S(2)}) %collective-permute-start.1) | collective-permute-done | bytes 163872 | tf_op jit(solution)/shard_map/ppermute | solution.py:483
  26.6 7.9 %spatial.2 = bf16[64,2,8,640]{3,2,1,0:T(8,128)(2,1)} custom-call(bf16[3,3,320,320]{3,2,1,0:T(8,128)(2,1)} %w_hbm.3, f32[320]{0:T(512)} %b_hbm.3, bf16[2,12,320,128]{3,2,1,0:T(8,128)(2,1)} %bitcast.6, bf16[2,1,320,128]{3,2,1,0:T(8,128)(2,1)S(1)} %collective-permute-done.low_hbm, bf16[2,1,320,128]{3,2,1,0:T(8,128)(2,1)S(1)} %collective-permute-done.1.high_hbm), custom_call_target="tpu_custom_call" | custom-call | flops 4400000000 | bytes 8000000 | tf_op jit(solution)/shard_map/spatial/pallas_call | solution.py:132
  34.5 0.0 copy-start.5
  34.5 0.0 copy-start.6
  34.5 0.0 copy-start.7
  34.5 0.0 copy-start.8
  34.5 0.0 copy-start
  34.5 0.0 copy-start.1
  34.5 0.0 copy-start.2
  34.6 0.0 copy-start.3
  34.6 3.3 %all-to-all-done.2.x_ref = bf16[64,1,8,640]{3,2,1,0:T(8,128)(2,1)S(1)} async-done(((bf16[64,1,8,640]{3,2,1,0:T(8,128)(2,1)}), bf16[64,1,8,640]{3,2,1,0:T(8,128)(2,1)S(1)}, u32[]{:S(2)}, u32[]{:S(2)}) %all-to-all-start.2) | async-done | bytes 655392 | tf_op jit(solution)/shard_map/all_to_all | solution.py:495
  37.8 6.5 %all-to-all-start = ((bf16[64,2,8,640]{3,2,1,0:T(8,128)(2,1)}), bf16[64,2,8,640]{3,2,1,0:T(8,128)(2,1)S(1)}, u32[]{:S(2)}, u32[]{:S(2)}) async-start(bf16[64,2,8,640]{3,2,1,0:T(8,128)(2,1)} %spatial.2), calls=%async_computation | async-start | bytes 2621440 | tf_op jit(solution)/shard_map/all_to_all | solution.py:495
  44.3 0.0 copy-done.5
  44.3 0.0 copy-done.6
  44.3 0.0 copy-done.7
  44.4 0.0 copy-done.8
  44.4 0.0 copy-done
  44.4 0.0 copy-done.1
  44.4 0.0 copy-done.2
  44.4 0.0 copy-done.3
  44.4 0.0 copy-start.4
  44.4 0.9 copy-done.4
  45.4 1.7 %prepare.1 = (bf16[1024,384]{1,0:T(8,128)(2,1)}, bf16[1024,384]{1,0:T(8,128)(2,1)}, bf16[384,1024]{1,0:T(8,128)(2,1)}, bf16[384,384]{1,0:T(8,128)(2,1)}) custom-call(bf16[3,320,320]{2,1,0:T(8,128)(2,1)S(1)} %copy-done, bf16[320,320]{1,0:T(8,128)(2,1)S(1)} %copy-done.1, bf16[320,320]{1,0:T(8,128)(2,1)S(1)} %copy-done.2, bf16[320,320]{1,0:T(8,128)(2,1)S(1)} %copy-done.3, ...), custom_call_target="tpu_custom_call" | custom-call | bytes 5000000 | tf_op jit(solution)/shard_map/prepare/pallas_call | solution.py:451
  47.1 8.8 %attend.3 = bf16[64,1,8,640]{3,2,1,0:T(8,128)(2,1)} custom-call(bf16[64,1,8,640]{3,2,1,0:T(8,128)(2,1)S(1)} %all-to-all-done.2.x_ref, bf16[1024,384]{1,0:T(8,128)(2,1)} %get-tuple-element.9.we_hbm, bf16[1024,384]{1,0:T(8,128)(2,1)} %get-tuple-element.10.wo_hbm, f32[8,384]{1,0:T(8,128)S(1)} %select_maximum_fusion.vector_ref, ...), custom_call_target="tpu_custom_call" | custom-call | flops 4000000000 | bytes 4000000 | tf_op jit(solution)/shard_map/attend/pallas_call | solution.py:342
  55.9 19.4 %all-to-all-done.x_ref = bf16[64,2,8,640]{3,2,1,0:T(8,128)(2,1)S(1)} async-done(((bf16[64,2,8,640]{3,2,1,0:T(8,128)(2,1)}), bf16[64,2,8,640]{3,2,1,0:T(8,128)(2,1)S(1)}, u32[]{:S(2)}, u32[]{:S(2)}) %all-to-all-start) | async-done | bytes 1310752 | tf_op jit(solution)/shard_map/all_to_all | solution.py:495
  75.3 5.2 %all-to-all-start.3 = ((bf16[64,1,8,640]{3,2,1,0:T(8,128)(2,1)}), bf16[64,1,8,640]{3,2,1,0:T(8,128)(2,1)S(1)}, u32[]{:S(2)}, u32[]{:S(2)}) async-start(bf16[64,1,8,640]{3,2,1,0:T(8,128)(2,1)} %attend.3), calls=%async_computation.3 | async-start | bytes 1310720 | tf_op jit(solution)/shard_map/all_to_all | solution.py:495
  80.5 15.8 %attend.2 = bf16[64,2,8,640]{3,2,1,0:T(8,128)(2,1)} custom-call(bf16[64,2,8,640]{3,2,1,0:T(8,128)(2,1)S(1)} %all-to-all-done.x_ref, bf16[1024,384]{1,0:T(8,128)(2,1)} %get-tuple-element.9.we_hbm, bf16[1024,384]{1,0:T(8,128)(2,1)} %get-tuple-element.10.wo_hbm, f32[8,384]{1,0:T(8,128)S(1)} %select_maximum_fusion.vector_ref, ...), custom_call_target="tpu_custom_call" | custom-call | flops 8000000000 | bytes 8000000 | tf_op jit(solution)/shard_map/attend/pallas_call | solution.py:342
  96.4 3.8 %all-to-all-done.3.x_ref = bf16[64,1,8,640]{3,2,1,0:T(8,128)(2,1)S(1)} async-done(((bf16[64,1,8,640]{3,2,1,0:T(8,128)(2,1)}), bf16[64,1,8,640]{3,2,1,0:T(8,128)(2,1)S(1)}, u32[]{:S(2)}, u32[]{:S(2)}) %all-to-all-start.3) | async-done | bytes 655392 | tf_op jit(solution)/shard_map/all_to_all | solution.py:495
  100.2 5.8 %all-to-all-start.1 = ((bf16[64,2,8,640]{3,2,1,0:T(8,128)(2,1)}), bf16[64,2,8,640]{3,2,1,0:T(8,128)(2,1)S(1)}, u32[]{:S(2)}, u32[]{:S(2)}) async-start(bf16[64,2,8,640]{3,2,1,0:T(8,128)(2,1)} %attend.2), calls=%async_computation.1 | async-start | bytes 2621440 | tf_op jit(solution)/shard_map/all_to_all | solution.py:495
  106.0 1.1 final.2.rest_0_
  107.0 32.2 %all-to-all-done.1.x_ref = bf16[64,2,8,640]{3,2,1,0:T(8,128)(2,1)S(1)} async-done(((bf16[64,2,8,640]{3,2,1,0:T(8,128)(2,1)}), bf16[64,2,8,640]{3,2,1,0:T(8,128)(2,1)S(1)}, u32[]{:S(2)}, u32[]{:S(2)}) %all-to-all-start.1) | async-done | bytes 1310752 | tf_op jit(solution)/shard_map/all_to_all | solution.py:495
  139.3 1.3 final.3
  (5 shorter events, 0.0 us)
Async XLA Ops:
  5.8 32.0 %all-to-all-start.2 = ((bf16[64,1,8,640]{3,2,1,0:T(8,128)(2,1)}), bf16[64,1,8,640]{3,2,1,0:T(8,128)(2,1)S(1)}, u32[]{:S(2)}, u32[]{:S(2)}) async-start(bf16[64,1,8,640]{3,2,1,0:T(8,128)(2,1)} %spatial.3), calls=%async_computation.2 | async-start | bytes 1310720 | tf_op jit(solution)/shard_map/all_to_all | solution.py:495
  17.3 2.6 %collective-permute-start = (bf16[2,1,320,128]{3,2,1,0:T(8,128)(2,1)S(1)}, bf16[2,1,320,128]{3,2,1,0:T(8,128)(2,1)S(1)}, u32[]{:S(2)}, u32[]{:S(2)}) collective-permute-start(bf16[2,1,320,128]{3,2,1,0:T(8,128)(2,1)S(1)} %get-tuple-element.14), channel_id=1, source_target_pairs={{0,1},{1,2},{2,3},{4,5},{5,6},{6,7},{8,9},{9,10},{10,11},{12,13},{... | collective-permute-start | bytes 491528 | tf_op jit(solution)/shard_map/ppermute | solution.py:482
  18.6 8.0 %collective-permute-start.1 = (bf16[2,1,320,128]{3,2,1,0:T(8,128)(2,1)S(1)}, bf16[2,1,320,128]{3,2,1,0:T(8,128)(2,1)S(1)}, u32[]{:S(2)}, u32[]{:S(2)}) collective-permute-start(bf16[2,1,320,128]{3,2,1,0:T(8,128)(2,1)S(1)} %get-tuple-element.13), channel_id=1, source_target_pairs={{1,0},{2,1},{3,2},{5,4},{6,5},{7,6},{9,8},{10,9},{11,10},{13,12},{... | collective-permute-start | bytes 491528 | tf_op jit(solution)/shard_map/ppermute | solution.py:483
  34.5 9.8 %copy-start.5 = (f32[320]{0:T(512)S(1)}, f32[320]{0:T(512)}, u32[]{:S(2)}) copy-start(f32[320]{0:T(512)} %param.16) | copy-start | bytes 3844
  34.5 9.8 %copy-start.6 = (f32[320]{0:T(512)S(1)}, f32[320]{0:T(512)}, u32[]{:S(2)}) copy-start(f32[320]{0:T(512)} %param.17) | copy-start | bytes 3844
  34.5 9.9 %copy-start.7 = (f32[320]{0:T(512)S(1)}, f32[320]{0:T(512)}, u32[]{:S(2)}) copy-start(f32[320]{0:T(512)} %param.18) | copy-start | bytes 3844
  34.5 9.9 %copy-start.8 = (f32[320]{0:T(512)S(1)}, f32[320]{0:T(512)}, u32[]{:S(2)}) copy-start(f32[320]{0:T(512)} %param.23) | copy-start | bytes 3844
  34.5 9.9 %copy-start = (bf16[3,320,320]{2,1,0:T(8,128)(2,1)S(1)}, bf16[3,320,320]{2,1,0:T(8,128)(2,1)}, u32[]{:S(2)}) copy-start(bf16[3,320,320]{2,1,0:T(8,128)(2,1)} %wt_ref.1) | copy-start | bytes 1843204
  34.5 9.9 %copy-start.1 = (bf16[320,320]{1,0:T(8,128)(2,1)S(1)}, bf16[320,320]{1,0:T(8,128)(2,1)}, u32[]{:S(2)}) copy-start(bf16[320,320]{1,0:T(8,128)(2,1)} %wq_ref.1) | copy-start | bytes 614404
  34.5 9.9 %copy-start.2 = (bf16[320,320]{1,0:T(8,128)(2,1)S(1)}, bf16[320,320]{1,0:T(8,128)(2,1)}, u32[]{:S(2)}) copy-start(bf16[320,320]{1,0:T(8,128)(2,1)} %wk_ref.1) | copy-start | bytes 614404
  34.6 9.9 %copy-start.3 = (bf16[320,320]{1,0:T(8,128)(2,1)S(1)}, bf16[320,320]{1,0:T(8,128)(2,1)}, u32[]{:S(2)}) copy-start(bf16[320,320]{1,0:T(8,128)(2,1)} %wv_ref.1) | copy-start | bytes 614404
  37.8 37.5 %all-to-all-start = ((bf16[64,2,8,640]{3,2,1,0:T(8,128)(2,1)}), bf16[64,2,8,640]{3,2,1,0:T(8,128)(2,1)S(1)}, u32[]{:S(2)}, u32[]{:S(2)}) async-start(bf16[64,2,8,640]{3,2,1,0:T(8,128)(2,1)} %spatial.2), calls=%async_computation | async-start | bytes 2621440 | tf_op jit(solution)/shard_map/all_to_all | solution.py:495
  44.4 0.9 copy-start.4
  75.3 24.9 %all-to-all-start.3 = ((bf16[64,1,8,640]{3,2,1,0:T(8,128)(2,1)}), bf16[64,1,8,640]{3,2,1,0:T(8,128)(2,1)S(1)}, u32[]{:S(2)}, u32[]{:S(2)}) async-start(bf16[64,1,8,640]{3,2,1,0:T(8,128)(2,1)} %attend.3), calls=%async_computation.3 | async-start | bytes 1310720 | tf_op jit(solution)/shard_map/all_to_all | solution.py:495
  100.2 39.1 %all-to-all-start.1 = ((bf16[64,2,8,640]{3,2,1,0:T(8,128)(2,1)}), bf16[64,2,8,640]{3,2,1,0:T(8,128)(2,1)S(1)}, u32[]{:S(2)}, u32[]{:S(2)}) async-start(bf16[64,2,8,640]{3,2,1,0:T(8,128)(2,1)} %attend.2), calls=%async_computation.1 | async-start | bytes 2621440 | tf_op jit(solution)/shard_map/all_to_all | solution.py:495
